TPU v7x, 32 devices: a whole 2x2x4 slice. The times are simulated.
32 devices in a mesh: fsdp: 32 (over z, y, x, core).
Axes of the slice: x: 2, y: 2, z: 4, core: 2. Of those that a mesh axis runs over, the one named last changes fastest.
Arguments:
- tokens: bfloat16 [65536, 640], P('fsdp'), may hold values from -6 to 6
- out_grad: bfloat16 [65536, 640], P('fsdp'), may hold values from -6 to 6
- seq_lengths: int32 [64, 4], P('fsdp'), may hold values from 0 to 1024, as said below
- w_query: bfloat16 [640, 1024], P(None, 'fsdp'), may hold values from -0.25 to 0.25
- w_key: bfloat16 [640, 256], P(None, 'fsdp'), may hold values from -0.25 to 0.25
- w_value: bfloat16 [640, 256], P(None, 'fsdp'), may hold values from -0.25 to 0.25
- w_output: bfloat16 [640, 1024], P(None, 'fsdp'), may hold values from -0.1875 to 0.1875
- w_gate: bfloat16 [640, 2048], P(None, 'fsdp'), may hold values from -0.25 to 0.25
- w_up: bfloat16 [640, 2048], P(None, 'fsdp'), may hold values from -0.25 to 0.25
- w_down: bfloat16 [640, 2048], P(None, 'fsdp'), may hold values from -0.125 to 0.125
- gain_input: float32 [640], replicated, may hold values from 0.25 to 1.75
- gain_query: float32 [256], replicated, may hold values from 0.25 to 1.75
- gain_key: float32 [256], replicated, may hold values from 0.25 to 1.75
- gain_attn: float32 [640], replicated, may hold values from 0.25 to 1.75
- gain_ffn_in: float32 [640], replicated, may hold values from 0.25 to 1.75
- gain_ffn_out: float32 [640], replicated, may hold values from 0.25 to 1.75
Outputs:
- output: bfloat16 [65536, 640], P('fsdp')
- grad_tokens: bfloat16 [65536, 640], P('fsdp')
- grad_w_query: float32 [640, 1024], P(None, 'fsdp')
- grad_w_key: float32 [640, 256], P(None, 'fsdp')
- grad_w_value: float32 [640, 256], P(None, 'fsdp')
- grad_w_output: float32 [640, 1024], P(None, 'fsdp')
- grad_w_gate: float32 [640, 2048], P(None, 'fsdp')
- grad_w_up: float32 [640, 2048], P(None, 'fsdp')
- grad_w_down: float32 [640, 2048], P(None, 'fsdp')
- grad_gain_input: float32 [640], replicated
- grad_gain_query: float32 [256], replicated
- grad_gain_key: float32 [256], replicated
- grad_gain_attn: float32 [640], replicated
- grad_gain_ffn_in: float32 [640], replicated
- grad_gain_ffn_out: float32 [640], replicated
Inputs may be any that keep to these rules, and one draw needn't show every extreme that they name: `seq_lengths`: row s lists the lengths of up to 4 sequences packed in order into slot s; zeros are empty entries and a row sums to at most 1024. In every draw some slot holds one sequence of exactly 1024 tokens.
All inputs are finite; a program needn't handle non-finite values.
Results may differ from a plain program's by a relative error of at most 0.015.
Values may be sent and summed in bfloat16 or wider, within the bound.
No kernel may reach another device: no remote copies, remote signals or barrier semaphores. Data moves between devices by JAX's collectives and lax.ppermute only.
A program may use at most 256 MiB of HBM per device.

v0:
```python
import math

import jax
import jax.numpy as jnp
from jax import lax
from jax.sharding import PartitionSpec as P

HEADS = 4
HEAD_DIM = 256


EPSILON = 1e-06
ROPE_BASE = 1000000.0
NEG_FILL = -1e30
QUERY_SCALE = 0.0625


def norm_rows(values, scales):
    return values * lax.rsqrt(jnp.mean(values * values, axis=-1, keepdims=True) + EPSILON) * scales


def norm_back(values, scales, upstream):
    inv_rms = lax.rsqrt(jnp.mean(values * values, axis=-1, keepdims=True) + EPSILON)
    scaled_up = upstream * scales
    grad_values = inv_rms * scaled_up - values * (inv_rms * inv_rms * inv_rms) * jnp.mean(
        scaled_up * values, axis=-1, keepdims=True
    )
    grad_scales = jnp.sum((upstream * values * inv_rms).reshape(-1, values.shape[-1]), axis=0)
    return (grad_values, grad_scales)


def rotate_half(values):
    middle = values.shape[-1] // 2
    return jnp.concatenate([-values[..., middle:], values[..., :middle]], axis=-1)


def rope_apply(values, cos_table, sin_table):
    return values * cos_table + rotate_half(values) * sin_table


def rope_back(upstream, cos_table, sin_table):
    return upstream * cos_table - rotate_half(upstream * sin_table)


def slot_layout(lengths, row_count):
    seq_ends = jnp.cumsum(lengths, dtype=jnp.int32)
    row_grid = lax.broadcasted_iota(jnp.int32, (row_count, lengths.shape[0]), 0)
    passed = row_grid >= seq_ends[None, :]
    segment = jnp.sum(passed.astype(jnp.int32), axis=1, dtype=jnp.int32)
    start_row = jnp.sum(jnp.where(passed, lengths[None, :], 0), axis=1, dtype=jnp.int32)
    position = lax.iota(jnp.int32, row_count) - start_row
    return (segment, position)


def rope_tables(position):
    freq_index = lax.iota(jnp.int32, HEAD_DIM // 2).astype(jnp.float32)
    inverse = jnp.exp(freq_index * (-2.0 * math.log(ROPE_BASE) / HEAD_DIM))
    phases = position.astype(jnp.float32)[:, None] * inverse[None, :]
    phases = jnp.concatenate([phases, phases], axis=1)
    return (jnp.cos(phases), jnp.sin(phases))


def contract_rows(left, right):
    return lax.dot_general(
        left, right, (((0,), (0,)), ((), ())), preferred_element_type=jnp.float32
    )


def contract_cols(left, right):
    return lax.dot_general(
        left, right, (((1,), (1,)), ((), ())), preferred_element_type=jnp.float32
    )


def block_mask(segment, block_start, block_end):
    query_rows = (
        lax.broadcasted_iota(jnp.int32, (block_end - block_start, block_end), 0) + block_start
    )
    key_rows = lax.broadcasted_iota(jnp.int32, (block_end - block_start, block_end), 1)
    return (segment[block_start:block_end, None] == segment[None, :block_end]) & (
        key_rows <= query_rows
    )


def attention_forward(query_bf, key_bf, value_bf, segment):
    row_count = query_bf.shape[0]
    block_rows = min(512, row_count)
    pieces = []
    log_totals = []
    for block_index in range(row_count // block_rows):
        block_start = block_index * block_rows
        block_end = block_start + block_rows
        scores = jnp.einsum(
            "qhd,kd->hqk",
            query_bf[block_start:block_end],
            key_bf[:block_end],
            preferred_element_type=jnp.float32,
        )
        allowed = block_mask(segment, block_start, block_end)
        scores = jnp.where(allowed[None], scores, NEG_FILL)
        row_max = jnp.max(scores, axis=-1, keepdims=True)
        exp_scores = jnp.exp(scores - row_max)
        row_sum = jnp.sum(exp_scores, axis=-1, keepdims=True)
        attn_probs = (exp_scores / row_sum).astype(jnp.bfloat16)
        pieces.append(
            jnp.einsum(
                "hqk,kd->qhd", attn_probs, value_bf[:block_end], preferred_element_type=jnp.float32
            )
        )
        log_totals.append(row_max + jnp.log(row_sum))
    return (jnp.concatenate(pieces, axis=0), log_totals)


def attention_backward(query_bf, key_bf, value_bf, log_totals, grad_attended, segment):
    row_count = query_bf.shape[0]
    block_rows = min(512, row_count)
    query_pieces = []
    grad_key = jnp.zeros((row_count, HEAD_DIM), jnp.float32)
    grad_value = jnp.zeros((row_count, HEAD_DIM), jnp.float32)
    for block_index in range(row_count // block_rows):
        block_start = block_index * block_rows
        block_end = block_start + block_rows
        query_part = query_bf[block_start:block_end]
        grad_part = grad_attended[block_start:block_end]
        scores = jnp.einsum(
            "qhd,kd->hqk", query_part, key_bf[:block_end], preferred_element_type=jnp.float32
        )
        allowed = block_mask(segment, block_start, block_end)
        scores = jnp.where(allowed[None], scores, NEG_FILL)
        attn_probs = jnp.exp(scores - log_totals[block_index])
        grad_probs = jnp.einsum(
            "qhd,kd->hqk", grad_part, value_bf[:block_end], preferred_element_type=jnp.float32
        )
        grad_scores = attn_probs * (
            grad_probs - jnp.sum(attn_probs * grad_probs, axis=-1, keepdims=True)
        )
        grad_scores_bf = grad_scores.astype(jnp.bfloat16)
        query_pieces.append(
            jnp.einsum(
                "hqk,kd->qhd",
                grad_scores_bf,
                key_bf[:block_end],
                preferred_element_type=jnp.float32,
            )
        )
        grad_key = grad_key.at[:block_end].add(
            jnp.einsum(
                "hqk,qhd->kd", grad_scores_bf, query_part, preferred_element_type=jnp.float32
            )
        )
        grad_value = grad_value.at[:block_end].add(
            jnp.einsum(
                "hqk,qhd->kd",
                attn_probs.astype(jnp.bfloat16),
                grad_part,
                preferred_element_type=jnp.float32,
            )
        )
    return (jnp.concatenate(query_pieces, axis=0), grad_key, grad_value)


def slot_forward(tokens_slot, weights_full, gain_set, segment, cos_table, sin_table):
    w_query, w_key, w_value, w_output, w_gate, w_up, w_down = weights_full
    gain_input, gain_query, gain_key, gain_attn, gain_ffn_in, gain_ffn_out = gain_set
    row_count = tokens_slot.shape[0]
    inputs = tokens_slot.astype(jnp.float32)
    normed = norm_rows(inputs, gain_input).astype(jnp.bfloat16)
    query_raw = jnp.dot(normed, w_query, preferred_element_type=jnp.float32).reshape(
        row_count, HEADS, HEAD_DIM
    )
    key_raw = jnp.dot(normed, w_key, preferred_element_type=jnp.float32)
    value_bf = jnp.dot(normed, w_value, preferred_element_type=jnp.float32).astype(jnp.bfloat16)
    query_bf = (
        rope_apply(norm_rows(query_raw, gain_query), cos_table[:, None], sin_table[:, None])
        * QUERY_SCALE
    ).astype(jnp.bfloat16)
    key_bf = rope_apply(norm_rows(key_raw, gain_key), cos_table, sin_table).astype(jnp.bfloat16)
    attended, log_totals = attention_forward(query_bf, key_bf, value_bf, segment)
    attended_bf = attended.reshape(row_count, HEADS * HEAD_DIM).astype(jnp.bfloat16)
    branch = contract_cols(attended_bf, w_output)
    middle = inputs + norm_rows(branch, gain_attn)
    ffn_in = norm_rows(middle, gain_ffn_in).astype(jnp.bfloat16)
    gate_pre = jnp.dot(ffn_in, w_gate, preferred_element_type=jnp.float32)
    up_pre = jnp.dot(ffn_in, w_up, preferred_element_type=jnp.float32)
    hidden_bf = (jax.nn.gelu(gate_pre, approximate=True) * up_pre).astype(jnp.bfloat16)
    ffn_out = contract_cols(hidden_bf, w_down)
    result = middle + norm_rows(ffn_out, gain_ffn_out)
    stored = (
        inputs,
        normed,
        query_raw,
        key_raw,
        query_bf,
        key_bf,
        value_bf,
        log_totals,
        attended_bf,
        branch,
        middle,
        ffn_in,
        gate_pre,
        up_pre,
        hidden_bf,
        ffn_out,
    )
    return (result, stored)


def slot_backward(stored, weights_full, gain_set, segment, cos_table, sin_table, upstream):
    w_query, w_key, w_value, w_output, w_gate, w_up, w_down = weights_full
    gain_input, gain_query, gain_key, gain_attn, gain_ffn_in, gain_ffn_out = gain_set
    (
        inputs,
        normed,
        query_raw,
        key_raw,
        query_bf,
        key_bf,
        value_bf,
        log_totals,
        attended_bf,
        branch,
        middle,
        ffn_in,
        gate_pre,
        up_pre,
        hidden_bf,
        ffn_out,
    ) = stored
    row_count = inputs.shape[0]
    grad_ffn_out, grad_gain_ffn_out = norm_back(ffn_out, gain_ffn_out, upstream)
    grad_ffn_bf = grad_ffn_out.astype(jnp.bfloat16)
    grad_w_down = contract_rows(grad_ffn_bf, hidden_bf)
    grad_hidden = jnp.dot(grad_ffn_bf, w_down, preferred_element_type=jnp.float32)
    unused_value, gelu_pullback = jax.vjp(
        lambda gate_in, up_in: jax.nn.gelu(gate_in, approximate=True) * up_in, gate_pre, up_pre
    )
    grad_gate, grad_up = gelu_pullback(grad_hidden)
    grad_gate_bf = grad_gate.astype(jnp.bfloat16)
    grad_up_bf = grad_up.astype(jnp.bfloat16)
    grad_w_gate = contract_rows(ffn_in, grad_gate_bf)
    grad_w_up = contract_rows(ffn_in, grad_up_bf)
    grad_ffn_in = contract_cols(grad_gate_bf, w_gate) + contract_cols(grad_up_bf, w_up)
    grad_middle_norm, grad_gain_ffn_in = norm_back(middle, gain_ffn_in, grad_ffn_in)
    grad_middle = upstream + grad_middle_norm
    grad_branch, grad_gain_attn = norm_back(branch, gain_attn, grad_middle)
    grad_branch_bf = grad_branch.astype(jnp.bfloat16)
    grad_w_output = contract_rows(grad_branch_bf, attended_bf)
    grad_attended = (
        jnp.dot(grad_branch_bf, w_output, preferred_element_type=jnp.float32)
        .astype(jnp.bfloat16)
        .reshape(row_count, HEADS, HEAD_DIM)
    )
    grad_query, grad_key, grad_value = attention_backward(
        query_bf, key_bf, value_bf, log_totals, grad_attended, segment
    )
    query_norm_grad = rope_back(grad_query * QUERY_SCALE, cos_table[:, None], sin_table[:, None])
    grad_query_raw, grad_gain_query = norm_back(query_raw, gain_query, query_norm_grad)
    grad_key_raw, grad_gain_key = norm_back(
        key_raw, gain_key, rope_back(grad_key, cos_table, sin_table)
    )
    query_grad_bf = grad_query_raw.reshape(row_count, HEADS * HEAD_DIM).astype(jnp.bfloat16)
    key_grad_bf = grad_key_raw.astype(jnp.bfloat16)
    value_grad_bf = grad_value.astype(jnp.bfloat16)
    grad_w_query = contract_rows(normed, query_grad_bf)
    grad_w_key = contract_rows(normed, key_grad_bf)
    grad_w_value = contract_rows(normed, value_grad_bf)
    grad_normed = (
        contract_cols(query_grad_bf, w_query)
        + contract_cols(key_grad_bf, w_key)
        + contract_cols(value_grad_bf, w_value)
    )
    grad_inputs_norm, grad_gain_input = norm_back(inputs, gain_input, grad_normed)
    grad_rows = (grad_middle + grad_inputs_norm).astype(jnp.bfloat16)
    matrix_grads = (
        grad_w_query,
        grad_w_key,
        grad_w_value,
        grad_w_output,
        grad_w_gate,
        grad_w_up,
        grad_w_down,
    )
    gain_grads = (
        grad_gain_input,
        grad_gain_query,
        grad_gain_key,
        grad_gain_attn,
        grad_gain_ffn_in,
        grad_gain_ffn_out,
    )
    return (grad_rows, matrix_grads, gain_grads)


def add_all(previous, addend):
    if previous is None:
        return addend
    return tuple((earlier + later for earlier, later in zip(previous, addend)))


def shards(
    tokens,
    out_grad,
    seq_lengths,
    w_query,
    w_key,
    w_value,
    w_output,
    w_gate,
    w_up,
    w_down,
    gain_input,
    gain_query,
    gain_key,
    gain_attn,
    gain_ffn_in,
    gain_ffn_out,
):
    gain_set = (gain_input, gain_query, gain_key, gain_attn, gain_ffn_in, gain_ffn_out)
    slot_count = seq_lengths.shape[0]
    row_count = tokens.shape[0] // slot_count
    result_rows = []
    token_grads = []
    matrix_totals = None
    gain_totals = None
    for slot_index in range(slot_count):
        row_start = slot_index * row_count
        segment, position = slot_layout(seq_lengths[slot_index], row_count)
        cos_table, sin_table = rope_tables(position)
        forward_weights = (
            lax.all_gather(w_query, "fsdp", axis=1, tiled=True),
            lax.all_gather(w_key, "fsdp", axis=1, tiled=True),
            lax.all_gather(w_value, "fsdp", axis=1, tiled=True),
            lax.all_gather(w_output, "fsdp", axis=1, tiled=True),
            lax.all_gather(w_gate, "fsdp", axis=1, tiled=True),
            lax.all_gather(w_up, "fsdp", axis=1, tiled=True),
            lax.all_gather(w_down, "fsdp", axis=1, tiled=True),
        )
        result, stored = slot_forward(
            tokens[row_start : row_start + row_count],
            forward_weights,
            gain_set,
            segment,
            cos_table,
            sin_table,
        )
        result_rows.append(result.astype(jnp.bfloat16))
        live = (segment < seq_lengths.shape[1]).astype(jnp.float32)
        upstream = out_grad[row_start : row_start + row_count].astype(jnp.float32) * live[:, None]
        backward_weights = (
            lax.all_gather(w_query, "fsdp", axis=1, tiled=True),
            lax.all_gather(w_key, "fsdp", axis=1, tiled=True),
            lax.all_gather(w_value, "fsdp", axis=1, tiled=True),
            lax.all_gather(w_output, "fsdp", axis=1, tiled=True),
            lax.all_gather(w_gate, "fsdp", axis=1, tiled=True),
            lax.all_gather(w_up, "fsdp", axis=1, tiled=True),
            lax.all_gather(w_down, "fsdp", axis=1, tiled=True),
        )
        grad_rows, matrix_grads, gain_grads = slot_backward(
            stored, backward_weights, gain_set, segment, cos_table, sin_table, upstream
        )
        token_grads.append(grad_rows)
        matrix_totals = add_all(matrix_totals, matrix_grads)
        gain_totals = add_all(gain_totals, gain_grads)
    sum_query, sum_key, sum_value, sum_output, sum_gate, sum_up, sum_down = matrix_totals
    matrix_totals = (
        lax.psum_scatter(sum_query, "fsdp", scatter_dimension=1, tiled=True),
        lax.psum_scatter(sum_key, "fsdp", scatter_dimension=1, tiled=True),
        lax.psum_scatter(sum_value, "fsdp", scatter_dimension=1, tiled=True),
        lax.psum_scatter(sum_output, "fsdp", scatter_dimension=1, tiled=True),
        lax.psum_scatter(sum_gate, "fsdp", scatter_dimension=1, tiled=True),
        lax.psum_scatter(sum_up, "fsdp", scatter_dimension=1, tiled=True),
        lax.psum_scatter(sum_down, "fsdp", scatter_dimension=1, tiled=True),
    )
    gain_first, gain_second, gain_third, gain_fourth, gain_fifth, gain_sixth = gain_totals
    gain_totals = lax.psum(
        (gain_first, gain_second, gain_third, gain_fourth, gain_fifth, gain_sixth), "fsdp"
    )
    return (
        (jnp.concatenate(result_rows, axis=0), jnp.concatenate(token_grads, axis=0))
        + tuple(matrix_totals)
        + tuple(gain_totals)
    )


def solution(mesh):
    placed = (
        P("fsdp", None),
        P("fsdp", None),
        P("fsdp", None),
        P(None, "fsdp"),
        P(None, "fsdp"),
        P(None, "fsdp"),
        P(None, "fsdp"),
        P(None, "fsdp"),
        P(None, "fsdp"),
        P(None, "fsdp"),
        P(),
        P(),
        P(),
        P(),
        P(),
        P(),
    )
    return jax.shard_map(
        shards,
        mesh=mesh,
        in_specs=placed,
        out_specs=(
            P("fsdp", None),
            P("fsdp", None),
            P(None, "fsdp"),
            P(None, "fsdp"),
            P(None, "fsdp"),
            P(None, "fsdp"),
            P(None, "fsdp"),
            P(None, "fsdp"),
            P(None, "fsdp"),
            P(),
            P(),
            P(),
            P(),
            P(),
            P(),
        ),
        check_vma=False,
    )
```

profile of v0, /device:TPU:0, one launch (start us, length us, event | category | flops | bytes accessed | tf_op | source)
XLA Modules:
  0.0 1306.7 jit_solution(3691360419759911710)
XLA Ops:
  13.0 44.3 %all_gather.15 = bf16[640,256]{0,1:T(8,128)(2,1)S(1)} all-gather(bf16[640,8]{0,1:T(8,128)(2,1)S(1)} %copy-done.145), channel_id=1, replica_groups=mesh['fsdp'=32] {'fsdp'}, dimensions={1}, use_global_device_ids=true | all-gather | bytes 337920 | tf_op jit(solution)/shard_map/all_gather | solution.py:332
  61.3 38.0 %all_gather.14 = bf16[640,256]{0,1:T(8,128)(2,1)S(1)} all-gather(bf16[640,8]{0,1:T(8,128)(2,1)S(1)} %copy-done.146), channel_id=1, replica_groups=mesh['fsdp'=32] {'fsdp'}, dimensions={1}, use_global_device_ids=true | all-gather | bytes 337920 | tf_op jit(solution)/shard_map/all_gather | solution.py:333
  199.7 8.9 fusion.219
  208.6 34.9 %all-gather.12.cloned.1.call-done = bf16[640,2048]{0,1:T(8,128)(2,1)} async-done(((bf16[640,64]{0,1:T(8,128)(2,1)}), bf16[640,2048]{0,1:T(8,128)(2,1)}) %all-gather.12.cloned.1.call-update) | async-done | bytes 2621456 | tf_op jit(solution)/shard_map/all_gather | solution.py:336
  243.5 10.4 multiply_convert_fusion.2
  254.0 49.1 %all-gather.14.cloned.1.call-done = bf16[640,2048]{0,1:T(8,128)(2,1)} async-done(((bf16[640,64]{0,1:T(8,128)(2,1)}), bf16[640,2048]{0,1:T(8,128)(2,1)}) %all-gather.14.cloned.1.call-update) | async-done | bytes 2621456 | tf_op jit(solution)/shard_map/all_gather | solution.py:337
  303.1 6.7 multiply_reduce_fusion.16
  313.3 7.6 multiply_convert_fusion.3
  321.0 5.6 multiply_reduce_fusion.19
  330.8 18.0 %multiply_convert_fusion.1 = (bf16[1024,2048]{1,0:T(8,128)(2,1)}, bf16[1024,2048]{1,0:T(8,128)(2,1)}) fusion(f32[1024,2048]{1,0:T(8,128)} %copy-done.173, f32[1024,2048]{1,0:T(8,128)} %get-tuple-element.306, bf16[640,2048]{0,1:T(8,128)(2,1)} %all-gather.14.cloned.1.call-done, f32[1024,640]{1,0:T(8,128)} %copy-done.80, ...), kind=kOutput, calls=%fused_computation.33 | convolution fusion | flops 2739929088 | bytes 31739904 | tf_op jit(solution)/shard_map/dot_general | solution.py:234
  348.9 6.3 fusion.220
  355.2 5.7 multiply_reduce_fusion.7
  360.9 14.1 %multiply_convert_fusion = (bf16[1024,2048]{1,0:T(8,128)(2,1)}, bf16[1024,2048]{1,0:T(8,128)(2,1)}) fusion(f32[1024,2048]{1,0:T(8,128)} %fusion.219, f32[1024,2048]{1,0:T(8,128)} %get-tuple-element.310, bf16[640,2048]{0,1:T(8,128)(2,1)} %all-gather.14.cloned.1.call-done, f32[1024,640]{1,0:T(8,128)S(1)} %get-tuple-element.312, ...), kind=kOutput, calls=%fused_computation.31 | convolution fusion | flops 2739929088 | bytes 31739904 | tf_op jit(solution)/shard_map/dot_general | solution.py:234
  375.0 8.0 fusion.223
  383.1 7.5 multiply_reduce_fusion.9
  422.2 7.2 fusion.180
  441.9 6.6 fusion.181
  479.0 6.1 convolution_add_fusion.3
  522.2 15.2 %multiply_reduce_fusion.1 = (f32[1024,4]{0,1:T(4,128)S(1)}, f32[1024,4]{0,1:T(4,128)S(1)}, f32[1024,4,256]{2,0,1:T(8,128)}, f32[1024,4,256]{2,0,1:T(8,128)}, f32...) fusion(f32[1024,4,256]{2,0,1:T(8,128)} %copy.227, f32[256]{0:T(256)S(1)} %copy-done.148, ...), kind=kLoop, calls=%fused_computation.113 | loop fusion | flops 14671872 | bytes 44073984 | tf_op jit(solution)/shard_map/reduce_sum | solution.py:25
  548.4 11.8 fusion.40
  566.3 7.4 fusion.191
  573.8 6.2 convolution_add_fusion
  580.1 6.2 fusion.227
  591.8 6.0 fusion.226
  621.1 5.6 reshape.888
  649.3 6.9 copy.285
  681.6 38.9 %all-reduce.6 = (f32[640]{0:T(1024)}, f32[256]{0:T(256)}, f32[256]{0:T(256)}, f32[640]{0:T(1024)}, f32[640]{0:T(1024)}, /*index=5*/f32[640]{0:T(1024)}) all-reduce(f32[640]{0:T(1024)S(1)} %add.440, f32[256]{0:T(256)S(1)} %add.441, f32[256]{0:T(256)S(1)} %add.442, f32[640]{0:T(1024)S(1)} %add.443, ...), channel_id=1, replica_groups=mesh['fsdp'=32] {'fsdp'}, use_global_device_ids=true, to_apply=%region_51.52 | all-reduce | flops 3072 | bytes 24576 | tf_op jit(solution)/shard_map/psum | solution.py:376
  732.4 6.4 reduce-scatter.8.cloned.1.call-done
  738.8 136.4 %reduce-scatter.6.cloned.1.call-done = f32[640,32]{0,1:T(8,128)} async-done(((f32[640,1024]{0,1:T(8,128)}), f32[640,32]{0,1:T(8,128)}) %reduce-scatter.6.cloned.1.call-update) | async-done | bytes 81936 | tf_op jit(solution)/shard_map/reduce_scatter | solution.py:367
  875.2 141.8 %reduce-scatter.14.cloned.1.call-done = f32[640,64]{0,1:T(8,128)} async-done(((f32[640,2048]{0,1:T(8,128)}), f32[640,64]{0,1:T(8,128)}) %reduce-scatter.14.cloned.1.call-update) | async-done | bytes 163856 | tf_op jit(solution)/shard_map/reduce_scatter | solution.py:373
  1017.0 141.6 %reduce-scatter.12.cloned.1.call-done = f32[640,64]{0,1:T(8,128)} async-done(((f32[640,2048]{0,1:T(8,128)}), f32[640,64]{0,1:T(8,128)}) %reduce-scatter.12.cloned.1.call-update) | async-done | bytes 163856 | tf_op jit(solution)/shard_map/reduce_scatter | solution.py:372
  1158.6 141.4 %reduce-scatter.10.cloned.1.call-done = f32[640,64]{0,1:T(8,128)} async-done(((f32[640,2048]{0,1:T(8,128)}), f32[640,64]{0,1:T(8,128)}) %reduce-scatter.10.cloned.1.call-update) | async-done | bytes 163856 | tf_op jit(solution)/shard_map/reduce_scatter | solution.py:371
  (569 shorter events, 333.8 us)
Async XLA Ops:
  7.2 50.7 %copy-start.7 = (bf16[2048,640]{1,0:T(8,128)(2,1)S(1)}, bf16[2048,640]{1,0:T(8,128)(2,1)}, u32[]{:S(2)}) copy-start(bf16[2048,640]{1,0:T(8,128)(2,1)} %param.40) | copy-start | bytes 7864324
  7.2 50.7 %copy-start.128 = (f32[640]{0:T(1024)S(1)}, f32[640]{0:T(1024)}, u32[]{:S(2)}) copy-start(f32[640]{0:T(1024)} %param.50) | copy-start | bytes 7684
  7.2 124.4 %all-gather.6.cloned.1.call-start = ((), (), s32[]{:S(2)}) async-start(), calls=%async_computation.5 | async-start | bytes 1351680 | tf_op jit(solution)/shard_map/all_gather | solution.py:331
  7.9 178.1 %all-gather.8.cloned.1.call-start = ((), (), s32[]{:S(2)}) async-start(), calls=%async_computation.6 | async-start | bytes 1351680 | tf_op jit(solution)/shard_map/all_gather | solution.py:334
  8.7 191.0 %all-gather.10.cloned.1.call-start = ((), (), s32[]{:S(2)}) async-start(), calls=%async_computation.7 | async-start | bytes 2703360 | tf_op jit(solution)/shard_map/all_gather | solution.py:335
  9.4 234.1 %all-gather.12.cloned.1.call-start = ((), (), s32[]{:S(2)}) async-start(), calls=%async_computation.8 | async-start | bytes 2703360 | tf_op jit(solution)/shard_map/all_gather | solution.py:336
  10.0 293.1 %all-gather.14.cloned.1.call-start = ((), (), s32[]{:S(2)}) async-start(), calls=%async_computation.9 | async-start | bytes 2703360 | tf_op jit(solution)/shard_map/all_gather | solution.py:337
  10.6 719.1 %all-reduce.10.cloned.1.call-start = ((), (), s32[]{:S(2)}) async-start(), calls=%async_computation.15 | async-start | bytes 2621440
  57.9 73.8 %copy-start.125 = (f32[1024]{0:T(1024)}, f32[1024]{0:T(1024)S(1)}, u32[]{:S(2)}) copy-start(f32[1024]{0:T(1024)S(1)} %get-tuple-element.330) | copy-start | bytes 12292
  57.9 84.5 %copy-start.123 = (f32[1024]{0:T(1024)}, f32[1024]{0:T(1024)S(1)}, u32[]{:S(2)}) copy-start(f32[1024]{0:T(1024)S(1)} %get-tuple-element.242) | copy-start | bytes 12292
  106.9 12.2 copy-start.58
  129.2 49.4 %copy-start.45 = (pred[512,512]{0,1:T(8,128)(4,1)}, pred[512,512]{0,1:T(8,128)(4,1)S(1)}, u32[]{:S(2)}) copy-start(pred[512,512]{0,1:T(8,128)(4,1)S(1)} %fusion.155) | copy-start | bytes 786436
  131.6 37.6 %copy-start.24 = (pred[512,1024]{0,1:T(8,128)(4,1)}, pred[512,1024]{0,1:T(8,128)(4,1)S(1)}, u32[]{:S(2)}) copy-start(pred[512,1024]{0,1:T(8,128)(4,1)S(1)} %get-tuple-element.272) | copy-start | bytes 1572868
  309.8 51.1 %copy-start.78 = (f32[1024,640]{1,0:T(8,128)}, f32[1024,640]{1,0:T(8,128)S(1)}, u32[]{:S(2)}) copy-start(f32[1024,640]{1,0:T(8,128)S(1)} %get-tuple-element.312) | copy-start | bytes 7864324
  309.8 51.1 %copy-start.134 = (f32[1024]{0:T(1024)}, f32[1024]{0:T(1024)S(1)}, u32[]{:S(2)}) copy-start(f32[1024]{0:T(1024)S(1)} %get-tuple-element.264) | copy-start | bytes 12292
  309.8 51.1 %copy-start.154 = (f32[1024]{0:T(1024)}, f32[1024]{0:T(1024)S(1)}, u32[]{:S(2)}) copy-start(f32[1024]{0:T(1024)S(1)} %get-tuple-element.263) | copy-start | bytes 12292
  330.8 30.1 %copy-start.158 = (f32[1024]{0:T(1024)}, f32[1024]{0:T(1024)S(1)}, u32[]{:S(2)}) copy-start(f32[1024]{0:T(1024)S(1)} %broadcast_multiply_fusion.13) | copy-start | bytes 12292
  330.8 18.1 %copy-start.160 = (f32[1024]{0:T(1024)}, f32[1024]{0:T(1024)S(1)}, u32[]{:S(2)}) copy-start(f32[1024]{0:T(1024)S(1)} %broadcast_multiply_fusion.17) | copy-start | bytes 12292
  422.2 12.0 slice-start.2
  450.5 12.3 copy-start.107
  452.4 12.6 copy-start.109
  457.3 17.8 %copy-start.31 = (f32[1024,256]{0,1:T(8,128)}, f32[1024,256]{0,1:T(8,128)S(1)}, u32[]{:S(2)}) copy-start(f32[1024,256]{0,1:T(8,128)S(1)} %get-tuple-element.228) | copy-start | bytes 3145732
  462.8 14.9 %copy-start.32 = (f32[1024,256]{0,1:T(8,128)}, f32[1024,256]{0,1:T(8,128)S(1)}, u32[]{:S(2)}) copy-start(f32[1024,256]{0,1:T(8,128)S(1)} %get-tuple-element.226) | copy-start | bytes 3145732
  468.4 270.4 %reduce-scatter.8.cloned.1.call-start = ((), (), s32[]{:S(2)}) async-start(), calls=%async_computation.11 | async-start | bytes 2703360 | tf_op jit(solution)/shard_map/reduce_scatter | solution.py:370
  485.1 390.1 %reduce-scatter.6.cloned.1.call-start = ((), (), s32[]{:S(2)}) async-start(), calls=%async_computation.10 | async-start | bytes 2703360 | tf_op jit(solution)/shard_map/reduce_scatter | solution.py:367
  548.4 11.8 copy-start.10
  565.7 451.4 %reduce-scatter.14.cloned.1.call-start = ((), (), s32[]{:S(2)}) async-start(), calls=%async_computation.14 | async-start | bytes 5406720 | tf_op jit(solution)/shard_map/reduce_scatter | solution.py:373
  580.0 578.6 %reduce-scatter.12.cloned.1.call-start = ((), (), s32[]{:S(2)}) async-start(), calls=%async_computation.13 | async-start | bytes 5406720 | tf_op jit(solution)/shard_map/reduce_scatter | solution.py:372
  591.7 708.3 %reduce-scatter.10.cloned.1.call-start = ((), (), s32[]{:S(2)}) async-start(), calls=%async_computation.12 | async-start | bytes 5406720 | tf_op jit(solution)/shard_map/reduce_scatter | solution.py:371
  661.7 8.4 copy-start.37
  678.2 42.3 %copy-start.139 = (f32[1024]{0:T(1024)S(1)}, f32[1024]{0:T(1024)}, u32[]{:S(2)}) copy-start(f32[1024]{0:T(1024)} %get-tuple-element.241) | copy-start | bytes 12292
  678.2 42.2 %copy-start.140 = (f32[1024]{0:T(1024)S(1)}, f32[1024]{0:T(1024)}, u32[]{:S(2)}) copy-start(f32[1024]{0:T(1024)} %get-tuple-element.331) | copy-start | bytes 12292
  (163 other events, 581.5 us)
Sparse Core Ops, SparseCore 0:
  10.9 57.0 all-gather.5
  70.9 53.3 all-gather.7
  127.1 56.8 all-gather.9
  186.7 56.8 all-gather.11
  246.2 56.8 all-gather.13
  468.5 130.5 all-reduce.9
  602.0 136.8 reduce-scatter.7
  741.7 133.4 reduce-scatter.5
  878.1 138.8 reduce-scatter.13
  1019.7 138.8 reduce-scatter.11
  1161.5 138.4 reduce-scatter.9
where the time goes:
time: 1310 us
  waiting for transfers between devices  655 us (50%)
  matrix products  259 us (20%)
  local copies, waits for them, and re-layouts  135 us (10%)
  blocking collectives  121 us (9%)
  other arithmetic  120 us (9%)
  between operations  16.2 us (1%)
    reduce_scatter x1, waiting for transfers between devices, shards(): lax.psum_scatter(sum_down, 'fsdp', scatter_dimension=1, tiled=True)  142 us
    reduce_scatter x1, waiting for transfers between devices, shards(): lax.psum_scatter(sum_up, 'fsdp', scatter_dimension=1, tiled=True)  142 us
    reduce_scatter x1, waiting for transfers between devices, shards(): lax.psum_scatter(sum_gate, 'fsdp', scatter_dimension=1, tiled=True)  141 us
    reduce_scatter x1, waiting for transfers between devices, shards(): lax.psum_scatter(sum_query, 'fsdp', scatter_dimension=1, tiled=True)  136 us
    dot_general x14, matrix products, contract_rows(): lax.dot_general(left, right, (((0,), (0,)), ((), ())), preferred_element_...  58 us
    dot_general x14, matrix products, contract_cols(): lax.dot_general(left, right, (((1,), (1,)), ((), ())), preferred_element_...  54.6 us
    all_gather x1, waiting for transfers between devices, shards(): lax.all_gather(w_down, 'fsdp', axis=1, tiled=True)  49.1 us
    all_gather x1, blocking collectives, shards(): lax.all_gather(w_key, 'fsdp', axis=1, tiled=True)  44.3 us
  transfers between devices with their start and end apart: 11, of which 7 were waited for; matrix products, arithmetic and copies ran while one was open for 26% of the time, Pallas kernels for 0%

commit v1 on v0

v1 whole, which is shorter than its diff:
```python
import functools
import math

import jax
import jax.numpy as jnp
from jax import lax
from jax.experimental import pallas as pl
from jax.experimental.pallas import tpu as pltpu
from jax.sharding import PartitionSpec as P

HEADS = 4
HEAD_DIM = 256
HALF = HEAD_DIM // 2
EPSILON = 1e-06
ROPE_BASE = 1000000.0
NEG_FILL = -1e30
QUERY_SCALE = 0.0625
GELU_C = math.sqrt(2.0 / math.pi)
GELU_A = 0.044715
BF = jnp.bfloat16
F32 = jnp.float32
QBLOCK = 256
ROW_BLOCK = 512
FF_CHUNK = 512
VMEM_LIMIT = 60 * 1024 * 1024


def dot_nn(a, b):
    return lax.dot_general(a, b, (((1,), (0,)), ((), ())), preferred_element_type=F32)


def dot_nt(a, b):
    return lax.dot_general(a, b, (((1,), (1,)), ((), ())), preferred_element_type=F32)


def dot_tn(a, b):
    return lax.dot_general(a, b, (((0,), (0,)), ((), ())), preferred_element_type=F32)


def inv_rms(v):
    return lax.rsqrt(jnp.mean(v * v, axis=-1, keepdims=True) + EPSILON)


def row_sum(v):
    return jnp.sum(v, axis=0, keepdims=True)


def params(limit=VMEM_LIMIT):
    return pltpu.CompilerParams(dimension_semantics=("arbitrary",), vmem_limit_bytes=limit)


def const_spec(shape):
    zeros = (0,) * len(shape)
    return pl.BlockSpec(shape, lambda i, *_: zeros, pipeline_mode=pl.Buffered(1))


def cost(flops, nbytes, trans=0):
    return pl.CostEstimate(flops=int(flops), bytes_accessed=int(nbytes), transcendentals=int(trans))


def qkv_kernel(x_ref, w_ref, gi_ref, gq_ref, gk_ref, cos_ref, sin_ref, q_ref, k_ref, v_ref, s_ref, n_ref):
    x = x_ref[...].astype(F32)
    normed = (x * inv_rms(x) * gi_ref[...]).astype(BF)
    n_ref[...] = normed
    cos = cos_ref[...]
    sin = sin_ref[...]
    width = HEADS * HEAD_DIM
    v_ref[...] = dot_nt(normed, w_ref[width + HEAD_DIM :, :]).astype(BF)
    lane = lax.broadcasted_iota(jnp.int32, s_ref.shape, 1)
    saved = jnp.zeros(s_ref.shape, F32)
    for h in range(HEADS + 1):
        raw = dot_nt(normed, w_ref[h * HEAD_DIM : (h + 1) * HEAD_DIM, :])
        inv = inv_rms(raw)
        saved = jnp.where(lane == h, inv, saved)
        gain = gq_ref[...] * QUERY_SCALE if h < HEADS else gk_ref[...]
        y = raw * inv * gain
        y1 = y[:, :HALF]
        y2 = y[:, HALF:]
        out = q_ref.at[h] if h < HEADS else k_ref
        out[:, :HALF] = (y1 * cos - y2 * sin).astype(BF)
        out[:, HALF:] = (y2 * cos + y1 * sin).astype(BF)
    s_ref[...] = saved


def qkv_call(x, w_qkv, gi, gq, gk, cos, sin):
    rows, d = x.shape
    b = ROW_BLOCK
    width = HEADS * HEAD_DIM
    row = lambda n: pl.BlockSpec((b, n), lambda i: (i, 0))
    return pl.pallas_call(
        qkv_kernel,
        grid=(rows // b,),
        in_specs=[row(d), const_spec(w_qkv.shape), const_spec((1, d)), const_spec((1, HEAD_DIM)),
                  const_spec((1, HEAD_DIM)), row(HALF), row(HALF)],
        out_specs=[pl.BlockSpec((HEADS, b, HEAD_DIM), lambda i: (0, i, 0)), row(HEAD_DIM), row(HEAD_DIM),
                   row(128), row(d)],
        out_shape=[jax.ShapeDtypeStruct((HEADS, rows, HEAD_DIM), BF), jax.ShapeDtypeStruct((rows, HEAD_DIM), BF),
                   jax.ShapeDtypeStruct((rows, HEAD_DIM), BF), jax.ShapeDtypeStruct((rows, 128), F32),
                   jax.ShapeDtypeStruct((rows, d), BF)],
        compiler_params=params(),
        cost_estimate=cost(2 * rows * d * (width + 2 * HEAD_DIM), 12 * rows * d),
        name="qkv_rows",
    )(x, w_qkv, gi, gq, gk, cos, sin)


def attend_kernel(blocks, first_ref, q_ref, k_ref, v_ref, start_ref, p_ref, o_ref):
    i = pl.program_id(0)
    qb = lax.rem(i, blocks)
    first = first_ref[i]
    count = qb + 1 - first
    m_rows = HEADS * QBLOCK
    for n in range(1, blocks + 1):

        @pl.when(count == n)
        def _():
            base = pl.multiple_of(first * QBLOCK, QBLOCK)
            window = pl.ds(base, n * QBLOCK)
            q = q_ref[...].reshape(m_rows, HEAD_DIM)
            scores = dot_nt(q, k_ref[window, :])
            col = lax.broadcasted_iota(jnp.int32, scores.shape, 1) + base
            row = lax.broadcasted_iota(jnp.int32, (QBLOCK, 1), 0) + qb * QBLOCK
            row = jnp.concatenate([row] * HEADS, axis=0)
            start = jnp.concatenate([start_ref[...]] * HEADS, axis=0)
            scores = jnp.where((col >= start) & (col <= row), scores, NEG_FILL)
            e = jnp.exp(scores - jnp.max(scores, axis=-1, keepdims=True))
            probs = (e * (1.0 / jnp.sum(e, axis=-1, keepdims=True))).astype(BF)
            p_ref[0, :, : n * QBLOCK] = probs
            out = dot_nn(probs, v_ref[window, :]).astype(BF)
            for h in range(HEADS):
                o_ref[:, h * HEAD_DIM : (h + 1) * HEAD_DIM] = out[h * QBLOCK : (h + 1) * QBLOCK]


def attend_call(first, q, k, v, start, slots):
    rows = k.shape[0]
    slot_rows = rows // slots
    blocks = slot_rows // QBLOCK
    width = HEADS * HEAD_DIM
    slot = pl.BlockSpec((slot_rows, HEAD_DIM), lambda i, *_: (i // blocks, 0))
    return pl.pallas_call(
        functools.partial(attend_kernel, blocks),
        grid_spec=pltpu.PrefetchScalarGridSpec(
            num_scalar_prefetch=1,
            grid=(slots * blocks,),
            in_specs=[pl.BlockSpec((HEADS, QBLOCK, HEAD_DIM), lambda i, *_: (0, i, 0)), slot, slot,
                      pl.BlockSpec((QBLOCK, 1), lambda i, *_: (i, 0))],
            out_specs=[pl.BlockSpec((1, HEADS * QBLOCK, slot_rows), lambda i, *_: (i, 0, 0)),
                       pl.BlockSpec((QBLOCK, width), lambda i, *_: (i, 0))],
        ),
        out_shape=[jax.ShapeDtypeStruct((slots * blocks, HEADS * QBLOCK, slot_rows), BF),
                   jax.ShapeDtypeStruct((rows, width), BF)],
        compiler_params=params(),
        cost_estimate=cost(4 * rows * slot_rows * width * 5 // 8, 2 * rows * slot_rows * HEADS + 8 * rows * width,
                           rows * slot_rows * HEADS * 5 // 8),
        name="attend_rows",
    )(first, q, k, v, start)


def ffn_kernel(slot_rows, total_ref, a_ref, x_ref, og_ref, wo_ref, wg_ref, wu_ref, wd_ref, ga_ref, gf_ref, go_ref,
               out_ref, hid_ref, gg_ref, gu_ref, fin_ref, gfo_ref, gb_ref, gatt_ref, gm_ref, dg_ref,
               gate_s, up_s, acc_s):
    i = pl.program_id(0)
    b = x_ref.shape[0]
    chunks = wg_ref.shape[0] // FF_CHUNK

    @pl.when(i == 0)
    def _():
        dg_ref[...] = jnp.zeros_like(dg_ref)

    branch = dot_nn(a_ref[...], wo_ref[...])
    s_b = inv_rms(branch)
    nb = branch * s_b
    middle = x_ref[...].astype(F32) + nb * ga_ref[...]
    s_m = inv_rms(middle)
    nm = middle * s_m
    ffn_in = (nm * gf_ref[...]).astype(BF)
    fin_ref[...] = ffn_in

    acc_s[...] = jnp.zeros_like(acc_s)

    def forward(c, carry):
        rows = pl.ds(pl.multiple_of(c * FF_CHUNK, FF_CHUNK), FF_CHUNK)
        gate = dot_nt(fin_ref[...], wg_ref[rows, :])
        up = dot_nt(fin_ref[...], wu_ref[rows, :])
        gate_s[c] = gate
        up_s[c] = up
        t = jnp.tanh(gate * (GELU_C + (GELU_C * GELU_A) * (gate * gate)))
        hidden = (0.5 * gate * (1.0 + t) * up).astype(BF)
        hid_ref[c] = hidden
        acc_s[...] += dot_nn(hidden, wd_ref[rows, :])
        return carry

    lax.fori_loop(0, chunks, forward, 0)
    ffn_out = acc_s[...]
    s_f = inv_rms(ffn_out)
    nf = ffn_out * s_f
    out_ref[...] = (middle + nf * go_ref[...]).astype(BF)

    per_slot = slot_rows // b
    row = lax.broadcasted_iota(jnp.int32, (b, 1), 0) + lax.rem(i, per_slot) * b
    live = row < total_ref[i // per_slot]
    upstream = jnp.where(live, og_ref[...].astype(F32), 0.0)
    dg_fo = row_sum(upstream * nf)
    scaled = upstream * go_ref[...]
    gfo = (s_f * (scaled - nf * jnp.mean(scaled * nf, axis=-1, keepdims=True))).astype(BF)
    gfo_ref[...] = gfo
    acc_s[...] = jnp.zeros_like(acc_s)

    def backward(c, carry):
        rows = pl.ds(pl.multiple_of(c * FF_CHUNK, FF_CHUNK), FF_CHUNK)
        gh = dot_nt(gfo_ref[...], wd_ref[rows, :])
        gate = gate_s[c]
        sq = gate * gate
        t = jnp.tanh(gate * (GELU_C + (GELU_C * GELU_A) * sq))
        half_t = 0.5 + 0.5 * t
        slope = half_t + (0.5 * gate) * (1.0 - t * t) * (GELU_C + (3.0 * GELU_C * GELU_A) * sq)
        gg = (gh * up_s[c] * slope).astype(BF)
        gu = (gh * (gate * half_t)).astype(BF)
        gg_ref[c] = gg
        gu_ref[c] = gu
        acc_s[...] += dot_nn(gg, wg_ref[rows, :]) + dot_nn(gu, wu_ref[rows, :])
        return carry

    lax.fori_loop(0, chunks, backward, 0)
    gfin = acc_s[...]
    dg_fi = row_sum(gfin * nm)
    scaled = gfin * gf_ref[...]
    gm = upstream + s_m * (scaled - nm * jnp.mean(scaled * nm, axis=-1, keepdims=True))
    gm_ref[...] = gm
    dg_at = row_sum(gm * nb)
    scaled = gm * ga_ref[...]
    gb = (s_b * (scaled - nb * jnp.mean(scaled * nb, axis=-1, keepdims=True))).astype(BF)
    gb_ref[...] = gb
    gatt_ref[...] = dot_nt(gb, wo_ref[...]).astype(BF)
    dg_ref[0:1, :] += dg_fo
    dg_ref[1:2, :] += dg_fi
    dg_ref[2:3, :] += dg_at


def ffn_call(total, attended, x, og, wo, wg, wu, wd, ga, gf, go, slots):
    rows, d = x.shape
    ff = wg.shape[0]
    width = wo.shape[0]
    b = ROW_BLOCK
    chunks = ff // FF_CHUNK
    row = lambda n: pl.BlockSpec((b, n), lambda i, *_: (i, 0))
    wide = pl.BlockSpec((chunks, b, FF_CHUNK), lambda i, *_: (0, i, 0))
    vec = const_spec((1, d))
    sds = jax.ShapeDtypeStruct
    return pl.pallas_call(
        functools.partial(ffn_kernel, rows // slots),
        grid_spec=pltpu.PrefetchScalarGridSpec(
            num_scalar_prefetch=1,
            grid=(rows // b,),
            in_specs=[row(width), row(d), row(d), const_spec(wo.shape), const_spec(wg.shape), const_spec(wu.shape),
                      const_spec(wd.shape), vec, vec, vec],
            out_specs=[row(d), wide, wide, wide, row(d), row(d), row(d), row(width), row(d),
                       pl.BlockSpec((8, d), lambda i, *_: (0, 0))],
            scratch_shapes=[pltpu.VMEM((chunks, b, FF_CHUNK), F32), pltpu.VMEM((chunks, b, FF_CHUNK), F32),
                            pltpu.VMEM((b, d), F32)],
        ),
        out_shape=[sds((rows, d), BF), sds((chunks, rows, FF_CHUNK), BF), sds((chunks, rows, FF_CHUNK), BF),
                   sds((chunks, rows, FF_CHUNK), BF), sds((rows, d), BF), sds((rows, d), BF), sds((rows, d), BF),
                   sds((rows, width), BF), sds((rows, d), F32), sds((8, d), F32)],
        compiler_params=params(),
        cost_estimate=cost(4 * rows * d * (width + 3 * ff), rows * (6 * ff + 12 * d), 2 * rows * ff),
        name="ffn_rows",
    )(total, attended, x, og, wo, wg, wu, wd, ga, gf, go)


def rope_back_halves(g1, g2, cos, sin):
    return g1 * cos + g2 * sin, g2 * cos - g1 * sin


def norm_rope_back(grad, rotated, inv, gain, cos, sin, scale):
    m = jnp.mean(grad * rotated, axis=-1, keepdims=True)
    dy1, dy2 = rope_back_halves(grad[:, :HALF], grad[:, HALF:], cos, sin)
    u1, u2 = rope_back_halves(rotated[:, :HALF], rotated[:, HALF:], cos, sin)
    dy = jnp.concatenate([dy1, dy2], axis=1) * scale
    n = jnp.concatenate([u1, u2], axis=1) * ((1.0 / scale) / gain)
    return inv * (dy * gain - n * m), row_sum(dy * n)


def attend_back_kernel(blocks, first_ref, p_ref, q_ref, k_ref, v_ref, do_ref, s_ref, cos_ref, sin_ref, gq_ref, gk_ref,
                       gqr_ref, gkr_ref, gv_ref, dg_ref, dq_s, dk_s, dv_s):
    i = pl.program_id(0)
    qb = lax.rem(i, blocks)
    first = first_ref[i]
    count = qb + 1 - first
    m_rows = HEADS * QBLOCK

    @pl.when(i == 0)
    def _():
        dg_ref[...] = jnp.zeros_like(dg_ref)

    @pl.when(qb == 0)
    def _():
        dk_s[...] = jnp.zeros_like(dk_s)
        dv_s[...] = jnp.zeros_like(dv_s)

    for n in range(1, blocks + 1):

        @pl.when(count == n)
        def _():
            base = pl.multiple_of(first * QBLOCK, QBLOCK)
            window = pl.ds(base, n * QBLOCK)
            do = jnp.concatenate([do_ref[:, h * HEAD_DIM : (h + 1) * HEAD_DIM] for h in range(HEADS)], axis=0)
            q = q_ref[...].reshape(m_rows, HEAD_DIM)
            probs = p_ref[0, :, : n * QBLOCK]
            dp = dot_nt(do, v_ref[window, :])
            pf = probs.astype(F32)
            total = jnp.sum(pf * dp, axis=-1, keepdims=True)
            ds = (pf * (dp - total)).astype(BF)
            dq_s[...] = dot_nn(ds, k_ref[window, :])
            dk_s[window, :] += dot_tn(ds, q)
            dv_s[window, :] += dot_tn(probs, do)

    rows = pl.ds(pl.multiple_of(qb * QBLOCK, QBLOCK), QBLOCK)
    cos = cos_ref[rows, :]
    sin = sin_ref[rows, :]
    inv = s_ref[rows, :]
    for h in range(HEADS):
        grad, dg = norm_rope_back(dq_s[h * QBLOCK : (h + 1) * QBLOCK, :], q_ref[h].astype(F32), inv[:, h : h + 1],
                                  gq_ref[...], cos, sin, QUERY_SCALE)
        gqr_ref[:, h * HEAD_DIM : (h + 1) * HEAD_DIM] = grad.astype(BF)
        dg_ref[0:1, :] += dg

    @pl.when(qb == blocks - 1)
    def _():
        gv_ref[...] = dv_s[...].astype(BF)
        grad, dg = norm_rope_back(dk_s[...], k_ref[...].astype(F32), s_ref[:, HEADS : HEADS + 1], gk_ref[...],
                                  cos_ref[...], sin_ref[...], 1.0)
        gkr_ref[...] = grad.astype(BF)
        dg_ref[1:2, :] += dg


def attend_back_call(first, p, q, k, v, do, s, cos, sin, gq, gk, slots):
    rows = k.shape[0]
    slot_rows = rows // slots
    blocks = slot_rows // QBLOCK
    width = HEADS * HEAD_DIM
    slot = lambda n: pl.BlockSpec((slot_rows, n), lambda i, *_: (i // blocks, 0))
    block = lambda n: pl.BlockSpec((QBLOCK, n), lambda i, *_: (i, 0))
    sds = jax.ShapeDtypeStruct
    return pl.pallas_call(
        functools.partial(attend_back_kernel, blocks),
        grid_spec=pltpu.PrefetchScalarGridSpec(
            num_scalar_prefetch=1,
            grid=(slots * blocks,),
            in_specs=[pl.BlockSpec((1, HEADS * QBLOCK, slot_rows), lambda i, *_: (i, 0, 0)),
                      pl.BlockSpec((HEADS, QBLOCK, HEAD_DIM), lambda i, *_: (0, i, 0)),
                      slot(HEAD_DIM), slot(HEAD_DIM), block(width), slot(128), slot(HALF), slot(HALF),
                      const_spec((1, HEAD_DIM)), const_spec((1, HEAD_DIM))],
            out_specs=[block(width), slot(HEAD_DIM), slot(HEAD_DIM), pl.BlockSpec((8, HEAD_DIM), lambda i, *_: (0, 0))],
            scratch_shapes=[pltpu.VMEM((HEADS * QBLOCK, HEAD_DIM), F32), pltpu.VMEM((slot_rows, HEAD_DIM), F32),
                            pltpu.VMEM((slot_rows, HEAD_DIM), F32)],
        ),
        out_shape=[sds((rows, width), BF), sds((rows, HEAD_DIM), BF), sds((rows, HEAD_DIM), BF),
                   sds((8, HEAD_DIM), F32)],
        compiler_params=params(),
        cost_estimate=cost(8 * rows * slot_rows * width * 5 // 8, 2 * rows * slot_rows * HEADS + 12 * rows * width),
        name="attend_back_rows",
    )(first, p, q, k, v, do, s, cos, sin, gq, gk)


def input_back_kernel(gq_ref, gk_ref, gv_ref, x_ref, gm_ref, w_ref, gi_ref, gx_ref, dg_ref):
    @pl.when(pl.program_id(0) == 0)
    def _():
        dg_ref[...] = jnp.zeros_like(dg_ref)

    width = HEADS * HEAD_DIM
    gn = dot_nn(gq_ref[...], w_ref[:width, :])
    gn += dot_nn(gk_ref[...], w_ref[width : width + HEAD_DIM, :])
    gn += dot_nn(gv_ref[...], w_ref[width + HEAD_DIM :, :])
    x = x_ref[...].astype(F32)
    inv = inv_rms(x)
    n = x * inv
    dg_ref[0:1, :] += row_sum(gn * n)
    scaled = gn * gi_ref[...]
    gx = inv * (scaled - n * jnp.mean(scaled * n, axis=-1, keepdims=True))
    gx_ref[...] = (gm_ref[...] + gx).astype(BF)


def input_back_call(gq, gk, gv, x, gm, w_qkv, gi):
    rows, d = x.shape
    b = ROW_BLOCK
    row = lambda n: pl.BlockSpec((b, n), lambda i: (i, 0))
    return pl.pallas_call(
        input_back_kernel,
        grid=(rows // b,),
        in_specs=[row(gq.shape[1]), row(HEAD_DIM), row(HEAD_DIM), row(d), row(d), const_spec(w_qkv.shape),
                  const_spec((1, d))],
        out_specs=[row(d), pl.BlockSpec((8, d), lambda i: (0, 0))],
        out_shape=[jax.ShapeDtypeStruct((rows, d), BF), jax.ShapeDtypeStruct((8, d), F32)],
        compiler_params=params(),
        cost_estimate=cost(2 * rows * d * w_qkv.shape[0], 14 * rows * d),
        name="input_back_rows",
    )(gq, gk, gv, x, gm, w_qkv, gi)


def level_list(count):
    levels = [(1, 2)]
    stride = 2
    while stride < count:
        size = 4 if count // stride >= 4 else 2
        levels.append((stride, size))
        stride *= size
    return levels[::-1]


def send(x, count, offset):
    return lax.ppermute(x, "fsdp", [(i, i ^ offset) for i in range(count)])


def gather_blocks(x, count):
    x = x[None]
    for stride, size in level_list(count):
        x = jnp.concatenate([x] + [send(x, count, k * stride) for k in range(1, size)], axis=0)
    return x


def block_offsets(count):
    offsets = [0]
    for stride, size in level_list(count):
        offsets = [o ^ (k * stride) for k in range(size) for o in offsets]
    return offsets


def scatter_blocks(g, count):
    for stride, size in level_list(count)[::-1]:
        g = g.reshape((size, g.shape[0] // size) + g.shape[1:])
        g16 = g.astype(BF)
        total = g[0].astype(F32)
        for k in range(1, size):
            total = total + send(g16[k], count, k * stride).astype(F32)
        g = total
    return g[0]


def sum_small(x, count):
    for stride, size in level_list(count)[::-1]:
        parts = [x] + [send(x, count, k * stride) for k in range(1, size)]
        x = functools.reduce(jnp.add, parts)
    return x


def slot_layout(lengths, row_count):
    seq_ends = jnp.cumsum(lengths, axis=1, dtype=jnp.int32)
    rows = lax.broadcasted_iota(jnp.int32, (lengths.shape[0], row_count), 1)
    passed = rows[:, :, None] >= seq_ends[:, None, :]
    start = jnp.sum(jnp.where(passed, lengths[:, None, :], 0), axis=2, dtype=jnp.int32)
    return start, rows - start, seq_ends[:, -1]


def shards(count, tokens, out_grad, seq_lengths, w_query, w_key, w_value, w_output, w_gate, w_up, w_down,
           gain_input, gain_query, gain_key, gain_attn, gain_ffn_in, gain_ffn_out):
    slots = seq_lengths.shape[0]
    rows, d = tokens.shape
    slot_rows = rows // slots
    me = lax.axis_index("fsdp")
    offsets = jnp.array(block_offsets(count), jnp.int32)
    inverse = [0] * count
    for j, o in enumerate(block_offsets(count)):
        inverse[o] = j
    inverse = jnp.array(inverse, jnp.int32)
    place = inverse[jnp.arange(count, dtype=jnp.int32) ^ me]
    owner = offsets ^ me

    nq, nk, nf = w_query.shape[1], w_key.shape[1], w_gate.shape[1]
    own_qkv = jnp.concatenate([w_query.T, w_key.T, w_value.T], axis=0)
    all_qkv = gather_blocks(own_qkv, count)
    all_out = gather_blocks(w_output.T, count)
    own_ffn = jnp.concatenate([w_gate.T, w_up.T, w_down.T], axis=0)
    all_ffn = gather_blocks(own_ffn, count)

    start, position, total = slot_layout(seq_lengths, slot_rows)
    inv_freq = jnp.exp(lax.iota(jnp.int32, HALF).astype(F32) * (-2.0 * math.log(ROPE_BASE) / HEAD_DIM))
    phases = position.reshape(rows, 1).astype(F32) * inv_freq[None, :]
    cos = jnp.cos(phases)
    sin = jnp.sin(phases)
    first = (start[:, ::QBLOCK] // QBLOCK).reshape(-1)
    start_col = start.reshape(rows, 1)
    gi, gq, gk = gain_input[None], gain_query[None], gain_key[None]

    all_qkv = all_qkv[place]
    w_qkv = jnp.concatenate(
        [all_qkv[:, :nq].reshape(-1, d), all_qkv[:, nq : nq + nk].reshape(-1, d), all_qkv[:, nq + nk :].reshape(-1, d)],
        axis=0,
    )
    q, k, v, s, normed = qkv_call(tokens, w_qkv, gi, gq, gk, cos, sin)
    p, attended = attend_call(first, q, k, v, start_col, slots)

    wo = all_out[place].reshape(-1, d)
    wg = all_ffn[:, :nf].reshape(-1, d)
    wu = all_ffn[:, nf : 2 * nf].reshape(-1, d)
    wd = all_ffn[:, 2 * nf :].reshape(-1, d)
    out, hid, gg, gu, fin, gfo, gb, gatt, gm, dg_ffn = ffn_call(
        total, attended, tokens, out_grad, wo, wg, wu, wd, gain_attn[None], gain_ffn_in[None], gain_ffn_out[None], slots
    )

    def wide_grad(a, b):
        return lax.dot_general(a, b, (((1,), (0,)), ((), ())), preferred_element_type=F32).astype(BF).reshape(count, nf, d)

    g_down = scatter_blocks(wide_grad(hid, gfo), count)
    g_gate = scatter_blocks(wide_grad(gg, fin), count)
    g_up = scatter_blocks(wide_grad(gu, fin), count)
    g_out = dot_tn(attended, gb).astype(BF).reshape(count, nq, d)
    g_out = scatter_blocks(g_out[owner], count)

    gqr, gkr, gv, dg_att = attend_back_call(first, p, q, k, v, gatt, s, cos, sin, gq, gk, slots)
    g_q = dot_tn(gqr, normed).astype(BF).reshape(count, nq, d)
    g_k = dot_tn(gkr, normed).astype(BF).reshape(count, nk, d)
    g_v = dot_tn(gv, normed).astype(BF).reshape(count, nk, d)
    g_qkv = jnp.concatenate([g_q, g_k, g_v], axis=1)[owner]
    g_qkv = scatter_blocks(g_qkv, count)

    grad_tokens, dg_in = input_back_call(gqr, gkr, gv, tokens, gm, w_qkv, gi)
    gains = jnp.concatenate([dg_in[0], dg_att[0], dg_att[1], dg_ffn[2], dg_ffn[1], dg_ffn[0]])
    gains = sum_small(gains.reshape(-1, 128), count).reshape(-1)
    h = HEAD_DIM
    return (
        out,
        grad_tokens,
        g_qkv[:nq].T,
        g_qkv[nq : nq + nk].T,
        g_qkv[nq + nk :].T,
        g_out.T,
        g_gate.T,
        g_up.T,
        g_down.T,
        gains[:d],
        gains[d : d + h],
        gains[d + h : d + 2 * h],
        gains[d + 2 * h : 2 * d + 2 * h],
        gains[2 * d + 2 * h : 3 * d + 2 * h],
        gains[3 * d + 2 * h :],
    )


def solution(mesh):
    split_rows = P("fsdp", None)
    split_cols = P(None, "fsdp")
    return jax.shard_map(
        functools.partial(shards, mesh.shape["fsdp"]),
        mesh=mesh,
        in_specs=(split_rows,) * 3 + (split_cols,) * 7 + (P(),) * 6,
        out_specs=(split_rows,) * 2 + (split_cols,) * 7 + (P(),) * 6,
        check_vma=False,
    )
```

time: 1310 us -> 452 us (0.35)
  waiting for transfers between devices: 655 us -> 87 us
  matrix products: 259 us -> 40.9 us
  Pallas kernels: 0 us -> 142 us
  blocking collectives: 121 us -> 0 us
  other arithmetic: 120 us -> 23 us
  starting transfers between devices: 0.44 us -> 97 us
  local copies, waits for them, and re-layouts: 135 us -> 55.3 us
  between operations: 16.2 us -> 1.6 us
    reduce_scatter x5 -> x0, waiting for transfers between devices: 568 us -> none  [the longest x1 142 us: shards(): lax.psum_scatter(sum_down, 'fsdp', scatter_dimension=1, tiled=True)]
    dot_general x66 -> x7, matrix products: 259 us -> 40.9 us  [the longest x3 27.5 us: wide_grad(): lax.dot_general(a, b, (((1,), (0,)), ((), ())), preferred_element_type=F32)]
    pallas_call x0 -> x5, Pallas kernels: none -> 142 us  [the longest x1 76.9 us: ffn_call(): pl.pallas_call(functools.partial(ffn_kernel, rows // slots), grid_spec=pl...]
    ppermute x0 -> x63, starting transfers between devices: none -> 97 us  [send(): return lax.ppermute(x, 'fsdp', [(i, i ^ offset) for i in range(count)])]
    ppermute x0 -> x63, waiting for transfers between devices: none -> 87 us  [send(): return lax.ppermute(x, 'fsdp', [(i, i ^ offset) for i in range(count)])]
    all_gather x5 -> x0, waiting for transfers between devices: 84 us -> none  [the longest x1 49.1 us: shards(): lax.all_gather(w_down, 'fsdp', axis=1, tiled=True)]
    all_gather x2 -> x0, blocking collectives: 82.2 us -> none  [the longest x1 44.3 us: shards(): lax.all_gather(w_key, 'fsdp', axis=1, tiled=True)]
    reduce_sum x14 -> x1, other arithmetic: 46.5 us -> 0.78 us  [slot_layout(): jnp.sum(jnp.where(passed, lengths[:, None, :], 0), axis=2, dtype=jnp.int32)]
  transfers between devices with their start and end apart: 11 -> 63, of which waited for: 7 -> 25; matrix products, arithmetic and copies ran while one was open for 26% -> 22% of each run, Pallas kernels for 0% -> 6%
where the time goes in v1:
time: 452 us; the launch traced here: 447 us
  Pallas kernels  142 us (31%)
  starting transfers between devices  97 us (21%)
  waiting for transfers between devices  87 us (19%)
  local copies, waits for them, and re-layouts  55.3 us (12%)
  matrix products  40.9 us (9%)
  other arithmetic  23 us (5%)
    ppermute x63, starting transfers between devices, send(): return lax.ppermute(x, 'fsdp', [(i, i ^ offset) for i in range(count)])  97 us
    ppermute x63, waiting for transfers between devices, send(): return lax.ppermute(x, 'fsdp', [(i, i ^ offset) for i in range(count)])  87 us
    pallas_call x1, Pallas kernels, ffn_call(): pl.pallas_call(functools.partial(ffn_kernel, rows // slots), grid_spec=pl...  76.9 us
    dot_general x3, matrix products, wide_grad(): lax.dot_general(a, b, (((1,), (0,)), ((), ())), preferred_element_type=F32)  27.5 us
    pallas_call x1, Pallas kernels, attend_back_call(): pl.pallas_call(functools.partial(attend_back_kernel, blocks), grid_spec=p...  26.6 us
    pallas_call x1, Pallas kernels, attend_call(): pl.pallas_call(functools.partial(attend_kernel, blocks), grid_spec=pltpu....  16.5 us
    unnamed x72, local copies, waits for them, and re-layouts  16.2 us
    dot_general x4, matrix products, dot_tn(): lax.dot_general(a, b, (((0,), (0,)), ((), ())), preferred_element_type=F32)  13.4 us
  transfers between devices with their start and end apart: 63, of which 25 were waited for; matrix products, arithmetic and copies ran while one was open for 22% of the time, Pallas kernels for 6%

profile of v1, /device:TPU:0, one launch (start us, length us, event | category | flops | bytes accessed | tf_op | source)
XLA Modules:
  0.0 447.2 jit_solution(4509452325962272106)
XLA Ops:
  1.8 3.1 collective-permute-start.14
  8.4 3.5 collective-permute-start.8
  17.1 9.0 %collective-permute-done.15 = bf16[1,192,640]{2,1,0:T(8,128)(2,1)S(1)} collective-permute-done((bf16[1,192,640]{2,1,0:T(8,128)(2,1)S(1)}, bf16[1,192,640]{2,1,0:T(8,128)(2,1)S(1)}, u32[]{:S(2)}, u32[]{:S(2)}) %collective-permute-start.15) | collective-permute-done | bytes 245792 | tf_op jit(solution)/shard_map/ppermute | solution.py:411
  34.6 4.0 collective-permute-start
  43.8 7.2 %collective-permute-done.17 = bf16[4,192,640]{2,1,0:T(8,128)(2,1)S(1)} collective-permute-done((bf16[4,192,640]{2,1,0:T(8,128)(2,1)S(1)}, bf16[4,192,640]{2,1,0:T(8,128)(2,1)S(1)}, u32[]{:S(2)}, u32[]{:S(2)}) %collective-permute-start.17) | collective-permute-done | bytes 983072 | tf_op jit(solution)/shard_map/ppermute | solution.py:411
  55.0 13.7 %collective-permute-done.18 = bf16[4,192,640]{2,1,0:T(8,128)(2,1)S(1)} collective-permute-done((bf16[4,192,640]{2,1,0:T(8,128)(2,1)S(1)}, bf16[4,192,640]{2,1,0:T(8,128)(2,1)S(1)}, u32[]{:S(2)}, u32[]{:S(2)}) %collective-permute-start.18) | collective-permute-done | bytes 983072 | tf_op jit(solution)/shard_map/ppermute | solution.py:411
  87.1 7.8 %collective-permute-done.4 = bf16[4,48,640]{2,1,0:T(8,128)(2,1)S(1)} collective-permute-done((bf16[4,48,640]{2,1,0:T(8,128)(2,1)S(1)}, bf16[4,48,640]{2,1,0:T(8,128)(2,1)S(1)}, u32[]{:S(2)}, u32[]{:S(2)}) %collective-permute-start.4) | collective-permute-done | bytes 245792 | tf_op jit(solution)/shard_map/ppermute | solution.py:411
  102.7 5.8 %multiply_sine_fusion = (f32[2048,128]{1,0:T(8,128)}, f32[2048,128]{1,0:T(8,128)}) fusion(f32[128]{0:T(128)S(1)} %multiply_exponential_fusion, f32[2048]{0:T(1024)S(1)} %bitcast.165), kind=kLoop, calls=%fused_computation.22 | loop fusion | flops 262144 | bytes 2105856 | tf_op jit(solution)/shard_map/sin | solution.py:479
  115.6 11.2 %qkv_rows.1 = (bf16[4,2048,256]{2,1,0:T(8,128)(2,1)}, bf16[2048,256]{1,0:T(8,128)(2,1)}, bf16[2048,256]{1,0:T(8,128)(2,1)}, f32[2048,128]{1,0:T(8,128)}, bf16[2048,640]{1,0:T(8,128)(2,1)}) custom-call(bf16[2048,640]{1,0:T(8,128)(2,1)} %x_ref.5, bf16[1536,640]{1,0:T(8,128)(2,1)} %pad_maximum_fusion.w_ref, f32[1,640]{1,0:T(1,128)} %broadcast_in_dim.53.gi_ref, ...), custom_call_target="tpu_custom_call" | custom-call | flops 4026531840 | bytes 15728640 | tf_op jit(solution)/shard_map/qkv_rows/pallas_call | solution.py:90
  126.8 16.5 %attend_rows.1 = (bf16[8,1024,1024]{2,1,0:T(8,128)(2,1)}, bf16[2048,1024]{1,0:T(8,128)(2,1)}) custom-call(s32[8]{0:T(128)} %reshape.262.first_ref, bf16[4,2048,256]{2,1,0:T(8,128)(2,1)} %get-tuple-element.38.q_ref, bf16[2048,256]{1,0:T(8,128)(2,1)} %get-tuple-element.39.k_ref, bf16[2048,256]{1,0:T(8,128)(2,1)} %get-tuple-element.40.v_ref, s32[2048,1]{1,0:T(8,128)} %bitcast.146), custom_call_target="tpu_custom_call" | custom-call | flops 5368709120 | bytes 33554432 | tf_op jit(solution)/shard_map/attend_rows/pallas_call | solution.py:139
  143.4 4.4 constant_dynamic-update-slice_fusion.37
  147.8 5.5 %fusion.58 = (bf16[32,64,640]{2,1,0:T(8,128)(2,1)}, bf16[32,64,640]{2,1,0:T(8,128)(2,1)}, bf16[32,64,640]{2,1,0:T(8,128)(2,1)}) fusion(bf16[32,192,640]{2,1,0:T(8,128)(2,1)} %constant_dynamic-update-slice_fusion.37), kind=kLoop, calls=%fused_computation.165 | loop fusion | bytes 15728640 | tf_op jit(solution)/shard_map/slice | solution.py:495
  153.3 76.9 %ffn_rows.1 = (bf16[2048,640]{1,0:T(8,128)(2,1)}, bf16[4,2048,512]{2,1,0:T(8,128)(2,1)}, bf16[4,2048,512]{2,1,0:T(8,128)(2,1)}, bf16[4,2048,512]{2,1,0:T(8,128)(...) custom-call(s32[2]{0:T(128)} %slice_reduce_fusion.4.total_ref, ...), custom_call_target="tpu_custom_call" | custom-call | flops 37580963840 | bytes 40894464 | tf_op jit(solution)/shard_map/ffn_rows/pallas_call | solution.py:249
  230.2 26.6 %attend_back_rows.1 = (bf16[2048,1024]{1,0:T(8,128)(2,1)}, bf16[2048,256]{1,0:T(8,128)(2,1)}, bf16[2048,256]{1,0:T(8,128)(2,1)}, f32[8,256]{1,0:T(8,128)}) custom-call(s32[8]{0:T(128)} %reshape.262.first_ref, bf16[8,1024,1024]{2,1,0:T(8,128)(2,1)} %get-tuple-element.43.p_ref, bf16[4,2048,256]{2,1,0:T(8,128)(2,1)} %get-tuple-element.38.q_ref, ...), custom_call_target="tpu_custom_call" | custom-call | flops 10737418240 | bytes 41943040 | tf_op jit(solution)/shard_map/attend_back_rows/pallas_call | solution.py:344
  256.8 6.6 %convolution_convert_fusion.1 = bf16[1024,640]{1,0:T(8,128)(2,1)S(1)} fusion(bf16[2048,1024]{1,0:T(8,128)(2,1)} %get-tuple-element.46.gq_ref, bf16[2048,640]{1,0:T(8,128)(2,1)} %get-tuple-element.51), kind=kOutput, calls=%fused_computation.21 | convolution fusion | flops 2685009920 | bytes 8126464 | tf_op jit(solution)/shard_map/dot_general | solution.py:37
  264.5 11.2 %input_back_rows.1 = (bf16[2048,640]{1,0:T(8,128)(2,1)}, f32[8,640]{1,0:T(8,128)}) custom-call(bf16[2048,1024]{1,0:T(8,128)(2,1)} %get-tuple-element.46.gq_ref, bf16[2048,256]{1,0:T(8,128)(2,1)} %get-tuple-element.47.gk_ref, bf16[2048,256]{1,0:T(8,128)(2,1)} %get-tuple-element.48.gv_ref, bf16[2048,640]{1,0:T(8,128)(2,1)} %x_ref.5, ...), custom_call_target="tpu_custom_call" | custom-call | flops 4026531840 | bytes 18350080 | tf_op jit(solution)/shard_map/input_back_rows/pallas_call | solution.py:387
  278.1 3.3 collective-permute-start.56
  281.4 10.1 %fusion.12 = bf16[4,512,640]{2,1,0:T(8,128)(2,1)S(1)} fusion(bf16[4,2048,512]{2,1,0:T(8,128)(2,1)} %get-tuple-element.56, bf16[2048,640]{1,0:T(8,128)(2,1)} %get-tuple-element.57), kind=kOutput, calls=%fused_computation.16 | convolution fusion | flops 5370019840 | bytes 13631488 | tf_op jit(solution)/shard_map/dot_general | solution.py:501
  293.3 10.0 %fusion.9 = bf16[4,512,640]{2,1,0:T(8,128)(2,1)S(1)} fusion(bf16[4,2048,512]{2,1,0:T(8,128)(2,1)} %get-tuple-element.55, bf16[2048,640]{1,0:T(8,128)(2,1)S(1)} %copy-done.21), kind=kOutput, calls=%fused_computation.15 | convolution fusion | flops 5370019840 | bytes 13631488 | tf_op jit(solution)/shard_map/dot_general | solution.py:501
  304.7 7.4 %fusion.6 = bf16[4,512,640]{2,1,0:T(8,128)(2,1)S(1)} fusion(bf16[4,2048,512]{2,1,0:T(8,128)(2,1)S(1)} %bitcast.174, bf16[2048,640]{1,0:T(8,128)(2,1)S(1)} %copy-done.21), kind=kOutput, calls=%fused_computation.14 | convolution fusion | flops 5370019840 | bytes 13631488 | tf_op jit(solution)/shard_map/dot_general | solution.py:501
  312.2 4.7 %convolution_convert_fusion = bf16[1024,640]{1,0:T(8,128)(2,1)} fusion(bf16[2048,1024]{1,0:T(8,128)(2,1)S(1)} %copy-done.19, bf16[2048,640]{1,0:T(8,128)(2,1)S(1)} %copy-done.20), kind=kOutput, calls=%fused_computation.20 | convolution fusion | flops 2685009920 | bytes 8126464 | tf_op jit(solution)/shard_map/dot_general | solution.py:37
  318.0 5.6 %collective-permute-start.57 = (f32[24,128]{1,0:T(8,128)S(1)}, f32[24,128]{1,0:T(8,128)S(1)}, u32[]{:S(2)}, u32[]{:S(2)}) collective-permute-start(f32[24,128]{1,0:T(8,128)S(1)} %bitcast_add_fusion), channel_id=1, source_target_pairs={{0,2},{1,3},{2,0},{3,1},{4,6},{5,7},{6,4},{7,5},{8,10},{9,11},{10,... | collective-permute-start | bytes 36872 | tf_op jit(solution)/shard_map/ppermute | solution.py:411
  323.6 3.0 collective-permute-start.58
  331.3 5.3 %collective-permute-start.60 = (f32[24,128]{1,0:T(8,128)S(1)}, f32[24,128]{1,0:T(8,128)S(1)}, u32[]{:S(2)}, u32[]{:S(2)}) collective-permute-start(f32[24,128]{1,0:T(8,128)S(1)} %add_add_fusion.1), channel_id=1, source_target_pairs={{0,8},{1,9},{2,10},{3,11},{4,12},{5,13},{6,14},{7,15},{8,0},{9,1},... | collective-permute-start | bytes 36872 | tf_op jit(solution)/shard_map/ppermute | solution.py:411
  354.8 3.2 collective-permute-done.29
  367.9 4.1 collective-permute-done.23
  372.1 3.8 collective-permute-start.34
  401.8 6.2 %collective-permute-done.51 = bf16[4,64,640]{2,1,0:T(8,128)(2,1)S(1)} collective-permute-done((bf16[4,64,640]{2,1,0:T(8,128)(2,1)S(1)}, bf16[4,64,640]{2,1,0:T(8,128)(2,1)S(1)}, u32[]{:S(2)}, u32[]{:S(2)}) %collective-permute-start.51) | collective-permute-done | bytes 327712 | tf_op jit(solution)/shard_map/ppermute | solution.py:411
  409.5 3.4 collective-permute-done.43
  415.9 6.1 %collective-permute-done.44 = bf16[4,64,640]{2,1,0:T(8,128)(2,1)S(1)} collective-permute-done((bf16[4,64,640]{2,1,0:T(8,128)(2,1)S(1)}, bf16[4,64,640]{2,1,0:T(8,128)(2,1)S(1)}, u32[]{:S(2)}, u32[]{:S(2)}) %collective-permute-start.44) | collective-permute-done | bytes 327712 | tf_op jit(solution)/shard_map/ppermute | solution.py:411
  428.8 3.5 collective-permute-done.37
  443.0 3.2 collective-permute-done.41
  (262 shorter events, 149.6 us)
Async XLA Ops:
  1.8 15.3 %collective-permute-start.14 = (bf16[1,192,640]{2,1,0:T(8,128)(2,1)S(1)}, bf16[1,192,640]{2,1,0:T(8,128)(2,1)S(1)}, u32[]{:S(2)}, u32[]{:S(2)}) collective-permute-start(bf16[1,192,640]{2,1,0:T(8,128)(2,1)S(1)} %maximum_bitcast_fusion), channel_id=1, source_target_pairs={{0,8},{1,9},{2,10},{3,11},{4,12},{5,13},{6,14},{7,15},{8,0},{9,1},... | collective-permute-start | bytes 737288 | tf_op jit(solution)/shard_map/ppermute | solution.py:411
  4.9 21.2 %collective-permute-start.15 = (bf16[1,192,640]{2,1,0:T(8,128)(2,1)S(1)}, bf16[1,192,640]{2,1,0:T(8,128)(2,1)S(1)}, u32[]{:S(2)}, u32[]{:S(2)}) collective-permute-start(bf16[1,192,640]{2,1,0:T(8,128)(2,1)S(1)} %maximum_bitcast_fusion), channel_id=1, source_target_pairs={{0,16},{1,17},{2,18},{3,19},{4,20},{5,21},{6,22},{7,23},{8,24},{9,... | collective-permute-start | bytes 737288 | tf_op jit(solution)/shard_map/ppermute | solution.py:411
  7.5 18.6 %collective-permute-start.16 = (bf16[1,192,640]{2,1,0:T(8,128)(2,1)S(1)}, bf16[1,192,640]{2,1,0:T(8,128)(2,1)S(1)}, u32[]{:S(2)}, u32[]{:S(2)}) collective-permute-start(bf16[1,192,640]{2,1,0:T(8,128)(2,1)S(1)} %maximum_bitcast_fusion), channel_id=1, source_target_pairs={{0,24},{1,25},{2,26},{3,27},{4,28},{5,29},{6,30},{7,31},{8,16},{9,... | collective-permute-start | bytes 737288 | tf_op jit(solution)/shard_map/ppermute | solution.py:411
  7.5 23.8 %collective-permute-start.7 = (bf16[1,32,640]{2,1,0:T(8,128)(2,1)}, bf16[1,32,640]{2,1,0:T(8,128)(2,1)S(1)}, u32[]{:S(2)}, u32[]{:S(2)}) collective-permute-start(bf16[1,32,640]{2,1,0:T(8,128)(2,1)} %bitcast.153), channel_id=1, source_target_pairs={{0,8},{1,9},{2,10},{3,11},{4,12},{5,13},{6,14},{7,15},{8,0},{9,1},... | collective-permute-start | bytes 122888 | tf_op jit(solution)/shard_map/ppermute | solution.py:411
  8.4 26.2 %collective-permute-start.8 = (bf16[1,32,640]{2,1,0:T(8,128)(2,1)}, bf16[1,32,640]{2,1,0:T(8,128)(2,1)S(1)}, u32[]{:S(2)}, u32[]{:S(2)}) collective-permute-start(bf16[1,32,640]{2,1,0:T(8,128)(2,1)} %bitcast.154), channel_id=1, source_target_pairs={{0,16},{1,17},{2,18},{3,19},{4,20},{5,21},{6,22},{7,23},{8,24},{9,... | collective-permute-start | bytes 122888 | tf_op jit(solution)/shard_map/ppermute | solution.py:411
  26.3 24.8 %collective-permute-start.17 = (bf16[4,192,640]{2,1,0:T(8,128)(2,1)S(1)}, bf16[4,192,640]{2,1,0:T(8,128)(2,1)S(1)}, u32[]{:S(2)}, u32[]{:S(2)}) collective-permute-start(bf16[4,192,640]{2,1,0:T(8,128)(2,1)S(1)} %pad_maximum_fusion.2), channel_id=1, source_target_pairs={{0,2},{1,3},{2,0},{3,1},{4,6},{5,7},{6,4},{7,5},{8,10},{9,11},{10,... | collective-permute-start | bytes 2949128 | tf_op jit(solution)/shard_map/ppermute | solution.py:411
  28.7 40.0 %collective-permute-start.18 = (bf16[4,192,640]{2,1,0:T(8,128)(2,1)S(1)}, bf16[4,192,640]{2,1,0:T(8,128)(2,1)S(1)}, u32[]{:S(2)}, u32[]{:S(2)}) collective-permute-start(bf16[4,192,640]{2,1,0:T(8,128)(2,1)S(1)} %pad_maximum_fusion.2), channel_id=1, source_target_pairs={{0,4},{1,5},{2,6},{3,7},{4,0},{5,1},{6,2},{7,3},{8,12},{9,13},{10,... | collective-permute-start | bytes 2949128 | tf_op jit(solution)/shard_map/ppermute | solution.py:411
  30.9 39.4 %collective-permute-start.19 = (bf16[4,192,640]{2,1,0:T(8,128)(2,1)S(1)}, bf16[4,192,640]{2,1,0:T(8,128)(2,1)S(1)}, u32[]{:S(2)}, u32[]{:S(2)}) collective-permute-start(bf16[4,192,640]{2,1,0:T(8,128)(2,1)S(1)} %pad_maximum_fusion.2), channel_id=1, source_target_pairs={{0,6},{1,7},{2,4},{3,5},{4,2},{5,3},{6,0},{7,1},{8,14},{9,15},{10,... | collective-permute-start | bytes 2949128 | tf_op jit(solution)/shard_map/ppermute | solution.py:411
  34.6 39.0 %collective-permute-start = (bf16[1,48,640]{2,1,0:T(8,128)(2,1)S(1)}, bf16[1,48,640]{2,1,0:T(8,128)(2,1)S(1)}, u32[]{:S(2)}, u32[]{:S(2)}) collective-permute-start(bf16[1,48,640]{2,1,0:T(8,128)(2,1)S(1)} %maximum_bitcast_fusion.1), channel_id=1, source_target_pairs={{0,8},{1,9},{2,10},{3,11},{4,12},{5,13},{6,14},{7,15},{8,0},{9,1},... | collective-permute-start | bytes 184328 | tf_op jit(solution)/shard_map/ppermute | solution.py:411
  38.6 37.4 %collective-permute-start.1 = (bf16[1,48,640]{2,1,0:T(8,128)(2,1)S(1)}, bf16[1,48,640]{2,1,0:T(8,128)(2,1)S(1)}, u32[]{:S(2)}, u32[]{:S(2)}) collective-permute-start(bf16[1,48,640]{2,1,0:T(8,128)(2,1)S(1)} %maximum_bitcast_fusion.1), channel_id=1, source_target_pairs={{0,16},{1,17},{2,18},{3,19},{4,20},{5,21},{6,22},{7,23},{8,24},{9,... | collective-permute-start | bytes 184328 | tf_op jit(solution)/shard_map/ppermute | solution.py:411
  51.0 24.9 %collective-permute-start.2 = (bf16[1,48,640]{2,1,0:T(8,128)(2,1)S(1)}, bf16[1,48,640]{2,1,0:T(8,128)(2,1)S(1)}, u32[]{:S(2)}, u32[]{:S(2)}) collective-permute-start(bf16[1,48,640]{2,1,0:T(8,128)(2,1)S(1)} %maximum_bitcast_fusion.1), channel_id=1, source_target_pairs={{0,24},{1,25},{2,26},{3,27},{4,28},{5,29},{6,30},{7,31},{8,16},{9,... | collective-permute-start | bytes 184328 | tf_op jit(solution)/shard_map/ppermute | solution.py:411
  71.8 71.6 %collective-permute-start.20 = (bf16[16,192,640]{2,1,0:T(8,128)(2,1)}, bf16[16,192,640]{2,1,0:T(8,128)(2,1)}, u32[]{:S(2)}, u32[]{:S(2)}) collective-permute-start(bf16[16,192,640]{2,1,0:T(8,128)(2,1)} %get-tuple-element.107), channel_id=1, source_target_pairs={{0,1},{1,0},{2,3},{3,2},{4,5},{5,4},{6,7},{7,6},{8,9},{9,8},{10,11... | collective-permute-start | bytes 11796488 | tf_op jit(solution)/shard_map/ppermute | solution.py:411
  73.6 22.9 %collective-permute-start.11 = (bf16[4,32,640]{2,1,0:T(8,128)(2,1)S(1)}, bf16[4,32,640]{2,1,0:T(8,128)(2,1)S(1)}, u32[]{:S(2)}, u32[]{:S(2)}) collective-permute-start(bf16[4,32,640]{2,1,0:T(8,128)(2,1)S(1)} %pad_maximum_fusion.4), channel_id=1, source_target_pairs={{0,4},{1,5},{2,6},{3,7},{4,0},{5,1},{6,2},{7,3},{8,12},{9,13},{10,... | collective-permute-start | bytes 491528 | tf_op jit(solution)/shard_map/ppermute | solution.py:411
  78.1 16.8 %collective-permute-start.4 = (bf16[4,48,640]{2,1,0:T(8,128)(2,1)S(1)}, bf16[4,48,640]{2,1,0:T(8,128)(2,1)S(1)}, u32[]{:S(2)}, u32[]{:S(2)}) collective-permute-start(bf16[4,48,640]{2,1,0:T(8,128)(2,1)S(1)} %pad_maximum_fusion.3), channel_id=1, source_target_pairs={{0,4},{1,5},{2,6},{3,7},{4,0},{5,1},{6,2},{7,3},{8,12},{9,13},{10,... | collective-permute-start | bytes 737288 | tf_op jit(solution)/shard_map/ppermute | solution.py:411
  80.1 17.1 %collective-permute-start.12 = (bf16[4,32,640]{2,1,0:T(8,128)(2,1)S(1)}, bf16[4,32,640]{2,1,0:T(8,128)(2,1)S(1)}, u32[]{:S(2)}, u32[]{:S(2)}) collective-permute-start(bf16[4,32,640]{2,1,0:T(8,128)(2,1)S(1)} %pad_maximum_fusion.4), channel_id=1, source_target_pairs={{0,6},{1,7},{2,4},{3,5},{4,2},{5,3},{6,0},{7,1},{8,14},{9,15},{10,... | collective-permute-start | bytes 491528 | tf_op jit(solution)/shard_map/ppermute | solution.py:411
  96.5 13.9 %collective-permute-start.6 = (bf16[16,48,640]{2,1,0:T(8,128)(2,1)}, bf16[16,48,640]{2,1,0:T(8,128)(2,1)S(1)}, u32[]{:S(2)}, u32[]{:S(2)}) collective-permute-start(bf16[16,48,640]{2,1,0:T(8,128)(2,1)} %get-tuple-element.136), channel_id=1, source_target_pairs={{0,1},{1,0},{2,3},{3,2},{4,5},{5,4},{6,7},{7,6},{8,9},{9,8},{10,11... | collective-permute-start | bytes 2949128 | tf_op jit(solution)/shard_map/ppermute | solution.py:411
  278.1 39.8 %collective-permute-start.56 = (f32[24,128]{1,0:T(8,128)S(1)}, f32[24,128]{1,0:T(8,128)S(1)}, u32[]{:S(2)}, u32[]{:S(2)}) collective-permute-start(f32[24,128]{1,0:T(8,128)S(1)} %bitcast.160), channel_id=1, source_target_pairs={{0,1},{1,0},{2,3},{3,2},{4,5},{5,4},{6,7},{7,6},{8,9},{9,8},{10,11... | collective-permute-start | bytes 36872 | tf_op jit(solution)/shard_map/ppermute | solution.py:411
  293.3 93.0 %collective-permute-start.49 = (bf16[16,64,640]{2,1,0:T(8,128)(2,1)}, bf16[16,64,640]{2,1,0:T(8,128)(2,1)}, u32[]{:S(2)}, u32[]{:S(2)}) collective-permute-start(bf16[16,64,640]{2,1,0:T(8,128)(2,1)} %bitcast.46), channel_id=1, source_target_pairs={{0,1},{1,0},{2,3},{3,2},{4,5},{5,4},{6,7},{7,6},{8,9},{9,8},{10,11... | collective-permute-start | bytes 3932168 | tf_op jit(solution)/shard_map/ppermute | solution.py:411
  304.6 87.2 %collective-permute-start.42 = (bf16[16,64,640]{2,1,0:T(8,128)(2,1)}, bf16[16,64,640]{2,1,0:T(8,128)(2,1)}, u32[]{:S(2)}, u32[]{:S(2)}) collective-permute-start(bf16[16,64,640]{2,1,0:T(8,128)(2,1)} %bitcast.41), channel_id=1, source_target_pairs={{0,1},{1,0},{2,3},{3,2},{4,5},{5,4},{6,7},{7,6},{8,9},{9,8},{10,11... | collective-permute-start | bytes 3932168 | tf_op jit(solution)/shard_map/ppermute | solution.py:411
  318.0 11.8 %collective-permute-start.57 = (f32[24,128]{1,0:T(8,128)S(1)}, f32[24,128]{1,0:T(8,128)S(1)}, u32[]{:S(2)}, u32[]{:S(2)}) collective-permute-start(f32[24,128]{1,0:T(8,128)S(1)} %bitcast_add_fusion), channel_id=1, source_target_pairs={{0,2},{1,3},{2,0},{3,1},{4,6},{5,7},{6,4},{7,5},{8,10},{9,11},{10,... | collective-permute-start | bytes 36872 | tf_op jit(solution)/shard_map/ppermute | solution.py:411
  331.3 15.8 %collective-permute-start.60 = (f32[24,128]{1,0:T(8,128)S(1)}, f32[24,128]{1,0:T(8,128)S(1)}, u32[]{:S(2)}, u32[]{:S(2)}) collective-permute-start(f32[24,128]{1,0:T(8,128)S(1)} %add_add_fusion.1), channel_id=1, source_target_pairs={{0,8},{1,9},{2,10},{3,11},{4,12},{5,13},{6,14},{7,15},{8,0},{9,1},... | collective-permute-start | bytes 36872 | tf_op jit(solution)/shard_map/ppermute | solution.py:411
  382.4 13.3 %collective-permute-start.35 = (bf16[16,64,640]{2,1,0:T(8,128)(2,1)S(1)}, bf16[16,64,640]{2,1,0:T(8,128)(2,1)S(1)}, u32[]{:S(2)}, u32[]{:S(2)}) collective-permute-start(bf16[16,64,640]{2,1,0:T(8,128)(2,1)S(1)} %bitcast.142), channel_id=1, source_target_pairs={{0,1},{1,0},{2,3},{3,2},{4,5},{5,4},{6,7},{7,6},{8,9},{9,8},{10,11... | collective-permute-start | bytes 3932168 | tf_op jit(solution)/shard_map/ppermute | solution.py:411
  390.2 17.7 %collective-permute-start.51 = (bf16[4,64,640]{2,1,0:T(8,128)(2,1)S(1)}, bf16[4,64,640]{2,1,0:T(8,128)(2,1)S(1)}, u32[]{:S(2)}, u32[]{:S(2)}) collective-permute-start(bf16[4,64,640]{2,1,0:T(8,128)(2,1)S(1)} %get-tuple-element.97), channel_id=1, source_target_pairs={{0,4},{1,5},{2,6},{3,7},{4,0},{5,1},{6,2},{7,3},{8,12},{9,13},{10,... | collective-permute-start | bytes 983048 | tf_op jit(solution)/shard_map/ppermute | solution.py:411
  391.7 16.2 %collective-permute-start.52 = (bf16[4,64,640]{2,1,0:T(8,128)(2,1)S(1)}, bf16[4,64,640]{2,1,0:T(8,128)(2,1)S(1)}, u32[]{:S(2)}, u32[]{:S(2)}) collective-permute-start(bf16[4,64,640]{2,1,0:T(8,128)(2,1)S(1)} %get-tuple-element.96), channel_id=1, source_target_pairs={{0,6},{1,7},{2,4},{3,5},{4,2},{5,3},{6,0},{7,1},{8,14},{9,15},{10,... | collective-permute-start | bytes 983048 | tf_op jit(solution)/shard_map/ppermute | solution.py:411
  393.7 19.3 %collective-permute-start.43 = (bf16[4,64,640]{2,1,0:T(8,128)(2,1)S(1)}, bf16[4,64,640]{2,1,0:T(8,128)(2,1)S(1)}, u32[]{:S(2)}, u32[]{:S(2)}) collective-permute-start(bf16[4,64,640]{2,1,0:T(8,128)(2,1)S(1)} %get-tuple-element.98), channel_id=1, source_target_pairs={{0,2},{1,3},{2,0},{3,1},{4,6},{5,7},{6,4},{7,5},{8,10},{9,11},{10,... | collective-permute-start | bytes 983048 | tf_op jit(solution)/shard_map/ppermute | solution.py:411
  395.7 26.3 %collective-permute-start.44 = (bf16[4,64,640]{2,1,0:T(8,128)(2,1)S(1)}, bf16[4,64,640]{2,1,0:T(8,128)(2,1)S(1)}, u32[]{:S(2)}, u32[]{:S(2)}) collective-permute-start(bf16[4,64,640]{2,1,0:T(8,128)(2,1)S(1)} %get-tuple-element.100), channel_id=1, source_target_pairs={{0,4},{1,5},{2,6},{3,7},{4,0},{5,1},{6,2},{7,3},{8,12},{9,13},{10,... | collective-permute-start | bytes 983048 | tf_op jit(solution)/shard_map/ppermute | solution.py:411
  398.9 23.1 %collective-permute-start.45 = (bf16[4,64,640]{2,1,0:T(8,128)(2,1)S(1)}, bf16[4,64,640]{2,1,0:T(8,128)(2,1)S(1)}, u32[]{:S(2)}, u32[]{:S(2)}) collective-permute-start(bf16[4,64,640]{2,1,0:T(8,128)(2,1)S(1)} %get-tuple-element.99), channel_id=1, source_target_pairs={{0,6},{1,7},{2,4},{3,5},{4,2},{5,3},{6,0},{7,1},{8,14},{9,15},{10,... | collective-permute-start | bytes 983048 | tf_op jit(solution)/shard_map/ppermute | solution.py:411
  407.9 19.0 %collective-permute-start.36 = (bf16[4,64,640]{2,1,0:T(8,128)(2,1)S(1)}, bf16[4,64,640]{2,1,0:T(8,128)(2,1)S(1)}, u32[]{:S(2)}, u32[]{:S(2)}) collective-permute-start(bf16[4,64,640]{2,1,0:T(8,128)(2,1)S(1)} %get-tuple-element.101), channel_id=1, source_target_pairs={{0,2},{1,3},{2,0},{3,1},{4,6},{5,7},{6,4},{7,5},{8,10},{9,11},{10,... | collective-permute-start | bytes 983048 | tf_op jit(solution)/shard_map/ppermute | solution.py:411
  407.9 24.4 %collective-permute-start.37 = (bf16[4,64,640]{2,1,0:T(8,128)(2,1)S(1)}, bf16[4,64,640]{2,1,0:T(8,128)(2,1)S(1)}, u32[]{:S(2)}, u32[]{:S(2)}) collective-permute-start(bf16[4,64,640]{2,1,0:T(8,128)(2,1)S(1)} %get-tuple-element.103), channel_id=1, source_target_pairs={{0,4},{1,5},{2,6},{3,7},{4,0},{5,1},{6,2},{7,3},{8,12},{9,13},{10,... | collective-permute-start | bytes 983048 | tf_op jit(solution)/shard_map/ppermute | solution.py:411
  412.9 19.5 %collective-permute-start.38 = (bf16[4,64,640]{2,1,0:T(8,128)(2,1)S(1)}, bf16[4,64,640]{2,1,0:T(8,128)(2,1)S(1)}, u32[]{:S(2)}, u32[]{:S(2)}) collective-permute-start(bf16[4,64,640]{2,1,0:T(8,128)(2,1)S(1)} %get-tuple-element.102), channel_id=1, source_target_pairs={{0,6},{1,7},{2,4},{3,5},{4,2},{5,3},{6,0},{7,1},{8,14},{9,15},{10,... | collective-permute-start | bytes 983048 | tf_op jit(solution)/shard_map/ppermute | solution.py:411
  421.9 12.9 %collective-permute-start.53 = (bf16[1,64,640]{2,1,0:T(8,128)(2,1)S(1)}, bf16[1,64,640]{2,1,0:T(8,128)(2,1)S(1)}, u32[]{:S(2)}, u32[]{:S(2)}) collective-permute-start(bf16[1,64,640]{2,1,0:T(8,128)(2,1)S(1)} %get-tuple-element.116), channel_id=1, source_target_pairs={{0,8},{1,9},{2,10},{3,11},{4,12},{5,13},{6,14},{7,15},{8,0},{9,1},... | collective-permute-start | bytes 245768 | tf_op jit(solution)/shard_map/ppermute | solution.py:411
  421.9 15.1 %collective-permute-start.54 = (bf16[1,64,640]{2,1,0:T(8,128)(2,1)S(1)}, bf16[1,64,640]{2,1,0:T(8,128)(2,1)S(1)}, u32[]{:S(2)}, u32[]{:S(2)}) collective-permute-start(bf16[1,64,640]{2,1,0:T(8,128)(2,1)S(1)} %get-tuple-element.118), channel_id=1, source_target_pairs={{0,16},{1,17},{2,18},{3,19},{4,20},{5,21},{6,22},{7,23},{8,24},{9,... | collective-permute-start | bytes 245768 | tf_op jit(solution)/shard_map/ppermute | solution.py:411
  (55 other events, 681.9 us)
